TPU v7x, 256 devices: a whole 4x4x8 slice. The times are simulated.
256 devices in a mesh: co: 32 (over y_hi, z, core), ci: 8 (over y_lo, x).
Axes of the slice: x: 4, y: 4 (y_hi: 2, y_lo: 2; y = y_hi * 2 + y_lo), z: 8, core: 2. Of those that a mesh axis runs over, the one named last changes fastest.
Arguments:
- features: bfloat16 [1024, 2048], P('ci'), may hold values from -6 to 6
- filter_bank: bfloat16 [27, 1024, 1024], P(None, 'co', 'ci'), may hold values from -0.0390625 to 0.0390625
- out_grad: bfloat16 [1024, 2048], P('co', 'ci'), may hold values from -6 to 6
Outputs:
- response: bfloat16 [1024, 2048], P('co', 'ci')
- in_grad: bfloat16 [1024, 2048], P('ci', 'co')
- filter_grad: float32 [27, 1024, 1024], P(None, 'co', 'ci')
All inputs are finite; a program needn't handle non-finite values.
Results may differ from a plain program's by a relative error of at most 0.001.
Values may be sent and summed in bfloat16 or wider, within the bound.
No kernel may reach another device: no remote copies, remote signals or barrier semaphores. Data moves between devices by JAX's collectives and lax.ppermute only.
A program may use at most 64 MiB of HBM per device.

v0:
```python
import jax
import jax.numpy as jnp
from jax import lax
from jax.experimental import pallas as pl
from jax.experimental.pallas import tpu as pltpu
from jax.sharding import PartitionSpec as P


NY = 8
NZ = 8
AREA = NY * NZ
LANES = 128
F32 = jnp.float32
BF16 = jnp.bfloat16


VMEM = pltpu.VMEM
SHIFTS = [(b, c) for b in (-1, 0, 1) for c in (-1, 0, 1)]


def in_vmem(n):
    return [pl.BlockSpec(memory_space=VMEM)] * n


def shift_rows(value, b, c):
    rows, lanes = value.shape
    if c:
        z = lax.broadcasted_iota(jnp.int32, value.shape, 0) % NZ
        rolled = pltpu.roll(value, (-c) % rows, 0)
        value = jnp.where(z == (NZ - 1 if c > 0 else 0), 0.0, rolled)
    if b:
        cube = value.reshape(rows // AREA, NY, NZ, lanes)
        edge = jnp.zeros((rows // AREA, 1, NZ, lanes), value.dtype)
        if b > 0:
            cube = jnp.concatenate([cube[:, 1:], edge], axis=1)
        else:
            cube = jnp.concatenate([edge, cube[:, :-1]], axis=1)
        value = cube.reshape(rows, lanes)
    return value


def position():
    co = lax.axis_index("co")
    return lax.rem(co, 2), lax.rem(co // 2, 2)


def pack_kernel(grad_ref, out_ref):
    tiles = []
    for t in range(2):
        tile = grad_ref[:, t * LANES:(t + 1) * LANES].astype(F32)
        tiles += [tile, pltpu.roll(tile, AREA, 1)]
    packed = jnp.concatenate(tiles, axis=0).T[:AREA].astype(BF16)
    for r in range(out_ref.shape[0]):
        out_ref[r] = packed


def response_kernel(x_ref, f_ref, out_ref, wide_ref, lhs, rhs):
    groups = out_ref.shape[0]
    planes = 4 * groups
    rows = groups * AREA
    width = 4 * LANES
    zero = jnp.zeros((AREA, LANES), BF16)
    rhs[192:, :] = jnp.zeros((AREA, 3 * width), BF16)
    for b in range(3):
        lhs[0:AREA, b * width:b * width + LANES] = zero
        lhs[2 * rows - AREA:2 * rows, (b + 1) * width - LANES:(b + 1) * width] = zero
        for c in range(3):
            for i in range(2):
                for j in range(4):
                    a = j - 1 - i
                    block = f_ref[(a + 1) * 9 + b * 3 + c] if -1 <= a <= 1 else jnp.zeros((32, LANES), BF16)
                    rhs[c * 64 + i * 32:c * 64 + (i + 1) * 32, b * width + j * LANES:b * width + (j + 1) * LANES] = block
    for pair in range(planes // 2):
        cells = x_ref[:, pair * LANES:(pair + 1) * LANES].astype(F32).T
        for b in range(3):
            moved = shift_rows(cells, b - 1, 0).astype(BF16)
            for i in range(2):
                piece = moved[i * AREA:(i + 1) * AREA]
                spots = [(pair, i + 1)]
                if i == 1 and pair + 1 < planes // 2:
                    spots.append((pair + 1, 0))
                if i == 0 and pair:
                    spots.append((pair - 1, 3))
                for p, j in spots:
                    at = (p % 2) * rows + (p // 2) * AREA
                    lhs[at:at + AREA, b * width + j * LANES:b * width + (j + 1) * LANES] = piece
    wide_ref[...] = lhs[:, width:2 * width]
    lane = lax.broadcasted_iota(jnp.int32, (rows, LANES), 1)
    parts = []
    for half in range(2):
        full = lax.dot_general(
            lhs[half * rows:(half + 1) * rows, :], rhs[...], (((1,), (1,)), ((), ())), preferred_element_type=F32
        )
        first = full[:, :LANES]
        last = full[:, LANES:]
        sides = shift_rows(first, 0, -1) + shift_rows(last, 0, 1)
        parts.append((sides, first))
    low = parts[0][0] + pltpu.roll(parts[0][1], AREA, 1)
    high = pltpu.roll(parts[1][0], AREA, 1) + parts[1][1]
    total = jnp.where(lane < AREA, low, high)
    core, _ = position()
    for g in range(groups):
        out_ref[lax.rem(g + core * (groups // 2), groups)] = total[g * AREA:(g + 1) * AREA]


def in_grad_kernel(mine_ref, other_ref, f0_ref, f1_ref, f2_ref, f3_ref, out_ref, lhs, rhs):
    groups = out_ref.shape[0]
    core, zpar = position()
    q = 2 * zpar + core
    rows = groups * AREA
    filters = (f0_ref, f1_ref, f2_ref, f3_ref)
    lane = lax.broadcasted_iota(jnp.int32, (rows, LANES), 1)
    own_lane = jnp.where(q == 0, jnp.where(lane >= 32, 1, 0), jnp.where(lane < 160 - 32 * q, 1, 0)) == 1
    back = lax.rem(160 - 32 * q, LANES)
    edge = jnp.zeros((AREA, LANES), F32)
    for source in range(4):
        ref = mine_ref if source < 2 else other_ref
        sel = lax.rem(zpar + core + source // 2 + source % 2, 2)
        block = ref[sel].reshape(rows, LANES).astype(F32)
        rolled = pltpu.roll(block, back, 1)
        below = jnp.concatenate([edge, rolled[:-AREA]], axis=0)
        above = jnp.concatenate([rolled[AREA:], edge], axis=0)
        near = jnp.where(own_lane, rolled, jnp.where(q == 0, below, above))
        for b in range(3):
            at = (b * 4 + source) * LANES
            lhs[:, at:at + LANES] = shift_rows(near, 1 - b, 0).astype(BF16)
            for c in range(3):
                for j in range(3):
                    rhs[at + j * 32:at + (j + 1) * 32, c * LANES:(c + 1) * LANES] = filters[source][(2 - j) * 9 + b * 3 + c]
                rhs[at + 96:at + LANES, c * LANES:(c + 1) * LANES] = jnp.zeros((32, LANES), BF16)
    full = jnp.dot(lhs[...], rhs[...], preferred_element_type=F32)
    total = shift_rows(full[:, :LANES], 0, 1) + full[:, LANES:2 * LANES] + shift_rows(full[:, 2 * LANES:], 0, -1)
    for k in range(groups):
        out_ref[lax.rem(k + (groups // 4) * q, groups)] = total[k * AREA:(k + 1) * AREA]


def filter_grad_kernel(mine_ref, wide_ref, out_ref, *, scale):
    groups = mine_ref.shape[1]
    rows = groups * AREA
    core, zpar = position()
    block = mine_ref[lax.rem(zpar + core, 2)].astype(F32).reshape(rows, LANES)
    turned = jnp.concatenate([block[k * LANES:(k + 1) * LANES].T for k in range(rows // LANES)], axis=1)
    turned = jnp.concatenate([turned[:64], turned[64:]], axis=1)
    cells = turned.shape[1]
    index = lax.broadcasted_iota(jnp.int32, turned.shape, 1)
    z = index % NZ
    y = (index // NZ) % NY
    wide = wide_ref[...]
    for s, (b, c) in enumerate(SHIFTS):
        moved = turned
        step = b * NZ + c
        if step:
            moved = pltpu.roll(turned, step % cells, 1)
        if c:
            moved = jnp.where(z == (0 if c > 0 else NZ - 1), 0.0, moved)
        if b:
            moved = jnp.where(y == (0 if b > 0 else NY - 1), 0.0, moved)
        full = jnp.dot(moved.astype(BF16), wide, preferred_element_type=F32)
        for a in (-1, 0, 1):
            total = full[:32, (a + 1) * LANES:(a + 2) * LANES] + full[32:, (a + 2) * LANES:(a + 3) * LANES]
            out_ref[(a + 1) * 9 + s] = total * scale


LIMIT = 20 * 2**20


def params():
    return pltpu.CompilerParams(vmem_limit_bytes=LIMIT)


def cost(flops, moved):
    return pl.CostEstimate(flops=flops, transcendentals=0, bytes_accessed=moved)


def pack(out_grad, receivers):
    return pl.pallas_call(
        pack_kernel,
        out_shape=jax.ShapeDtypeStruct((receivers, AREA, LANES), BF16),
        in_specs=in_vmem(1),
        out_specs=in_vmem(1)[0],
        compiler_params=params(),
        name="pack",
    )(out_grad)


def response_terms(features, bank):
    groups = features.shape[1] // (4 * AREA)
    rows = groups * AREA
    return pl.pallas_call(
        response_kernel,
        out_shape=(
            jax.ShapeDtypeStruct((groups, AREA, LANES), F32),
            jax.ShapeDtypeStruct((2 * rows, 4 * LANES), BF16),
        ),
        in_specs=in_vmem(2),
        out_specs=tuple(in_vmem(2)),
        scratch_shapes=[VMEM((2 * rows, 12 * LANES), BF16), VMEM((2 * LANES, 12 * LANES), BF16)],
        compiler_params=params(),
        cost_estimate=cost(2 * 27 * 32 * 128 * 2048, 2 * 10**6),
        name="response_terms",
    )(features, bank)


def in_grad_terms(mine, other, banks):
    groups = mine.shape[1]
    rows = groups * AREA
    return pl.pallas_call(
        in_grad_kernel,
        out_shape=jax.ShapeDtypeStruct((groups, AREA, LANES), F32),
        in_specs=in_vmem(6),
        out_specs=in_vmem(1)[0],
        scratch_shapes=[VMEM((rows, 12 * LANES), BF16), VMEM((12 * LANES, 3 * LANES), BF16)],
        compiler_params=params(),
        cost_estimate=cost(2 * 27 * 32 * 128 * 2048, 2 * 10**6),
        name="in_grad_terms",
    )(mine, other, *banks)


def filter_terms(mine, wide, scale):
    return pl.pallas_call(
        lambda *refs: filter_grad_kernel(*refs, scale=scale),
        out_shape=jax.ShapeDtypeStruct((27, 32, LANES), F32),
        in_specs=in_vmem(2),
        out_specs=in_vmem(1)[0],
        compiler_params=params(),
        cost_estimate=cost(2 * 27 * 32 * 128 * 2048, 2 * 10**6),
        name="filter_terms",
    )(mine, wide)


def body(features, bank, out_grad):
    cell_count = features.shape[1]
    n_ci = lax.axis_size("ci")
    n_co = lax.axis_size("co")
    other_z = [(i, i ^ 2) for i in range(n_co)]
    other_core = [(i, i ^ 1) for i in range(n_co)]
    gather_groups = [
        [(4 * k + 2 * ((h + c) % 2) + c) * n_ci + i for h in range(2) for i in range(n_ci)]
        for k in range(n_co // 4)
        for c in range(2)
    ]
    quads = n_co // 4
    sum_groups = [[4 * ((k - quads // 4 * q) % quads) + q for k in range(quads)] for q in range(4)]
    response_groups = [[o * n_ci + (i - o % 2 * n_ci // 2) % n_ci for i in range(n_ci)] for o in range(n_co)]
    packed = pack(out_grad, 2 * n_ci)
    mine = lax.all_to_all(packed, ("co", "ci"), 0, 0, tiled=True, axis_index_groups=gather_groups)
    mine = mine.reshape(2, n_ci, AREA, LANES)
    bank_z = lax.ppermute(bank, "co", other_z)
    bank_c = lax.ppermute(bank, "co", other_core)
    bank_cz = lax.ppermute(bank_z, "co", other_core)
    terms, wide = response_terms(features, bank)
    other = lax.ppermute(mine, "co", other_core)
    shares = in_grad_terms(mine, other, (bank, bank_z, bank_c, bank_cz))
    shares = lax.all_to_all(shares, "co", 0, 0, tiled=True, axis_index_groups=sum_groups)
    in_grad = jnp.sum(shares, axis=0).T.astype(BF16)
    terms = lax.all_to_all(terms, ("co", "ci"), 0, 0, tiled=True, axis_index_groups=response_groups)
    response = jnp.sum(terms, axis=0).reshape(AREA, 4, 32).transpose(2, 1, 0)
    response = response.reshape(32, 4 * AREA).astype(BF16)
    filter_grad = filter_terms(mine, wide, float(cell_count) ** (-0.5))
    return (response, in_grad, filter_grad)


def solution(mesh):
    placed = (P("ci", None), P(None, "co", "ci"), P("co", "ci"))
    return jax.shard_map(
        body,
        mesh=mesh,
        in_specs=placed,
        out_specs=(P("co", "ci"), P("ci", "co"), P(None, "co", "ci")),
        check_vma=False,
    )
```

profile of v0, /device:TPU:8, one launch (start us, length us, event | category | flops | bytes accessed | tf_op | source)
XLA Modules:
  0.0 54.0 jit_solution(2063708109016141662)
XLA Ops:
  0.6 0.0 copy-start
  0.6 0.7 %copy-done = bf16[32,256]{1,0:T(8,128)(2,1)S(1)} copy-done((bf16[32,256]{1,0:T(8,128)(2,1)S(1)}, bf16[32,256]{1,0:T(8,128)(2,1)}, u32[]{:S(2)}) %copy-start) | copy-done | bytes 16408
  1.3 0.0 copy-start.1
  1.4 0.9 %pack.1 = bf16[16,64,128]{2,1,0:T(8,128)(2,1)} custom-call(bf16[32,256]{1,0:T(8,128)(2,1)S(1)} %copy-done), custom_call_target="tpu_custom_call" | custom-call | tf_op jit(solution)/shard_map/pack/pallas_call | solution.py:176
  2.2 0.0 copy-start.2
  2.2 7.3 %all-to-all-start.1 = ((bf16[16,64,128]{2,1,0:T(8,128)(2,1)}), bf16[16,64,128]{2,1,0:T(8,128)(2,1)S(1)}, u32[]{:S(2)}, u32[]{:S(2)}) async-start(bf16[16,64,128]{2,1,0:T(8,128)(2,1)} %pack.1), calls=%async_computation.1 | async-start | bytes 524288 | tf_op jit(solution)/shard_map/all_to_all | solution.py:246
  9.5 0.0 copy-done.2
  9.5 1.6 %collective-permute-start.1 = (bf16[27,32,128]{2,1,0:T(8,128)(2,1)S(1)}, bf16[27,32,128]{2,1,0:T(8,128)(2,1)S(1)}, u32[]{:S(2)}, u32[]{:S(2)}) collective-permute-start(bf16[27,32,128]{2,1,0:T(8,128)(2,1)S(1)} %copy-done.2), channel_id=1, source_target_pairs={{0,16},{8,24},{16,0},{24,8},{32,48},{40,56},{48,32},{56,40},{64,80... | collective-permute-start | bytes 663560 | tf_op jit(solution)/shard_map/ppermute | solution.py:248
  11.0 6.2 %all-to-all-done.1 = bf16[16,64,128]{2,1,0:T(8,128)(2,1)S(1)} async-done(((bf16[16,64,128]{2,1,0:T(8,128)(2,1)}), bf16[16,64,128]{2,1,0:T(8,128)(2,1)S(1)}, u32[]{:S(2)}, u32[]{:S(2)}) %all-to-all-start.1) | async-done | bytes 262176 | tf_op jit(solution)/shard_map/all_to_all | solution.py:246
  17.2 0.0 collective-permute-start
  17.2 0.5 collective-permute-start.2
  17.8 0.2 collective-permute-done.1.f1_ref
  17.9 0.0 collective-permute-start.3
  17.9 0.0 copy-done.1
  17.9 2.3 %response_terms.1 = (f32[8,64,128]{2,1,0:T(8,128)}, bf16[1024,512]{1,0:T(8,128)(2,1)S(1)}) custom-call(bf16[128,2048]{1,0:T(8,128)(2,1)S(1)} %copy-done.1, bf16[27,32,128]{2,1,0:T(8,128)(2,1)S(1)} %copy-done.2), custom_call_target="tpu_custom_call" | custom-call | flops 452984832 | bytes 2000000 | tf_op jit(solution)/shard_map/response_terms/pallas_call | solution.py:189
  20.2 5.7 %all-to-all-start = ((f32[8,64,128]{2,1,0:T(8,128)}), f32[8,64,128]{2,1,0:T(8,128)S(1)}, u32[]{:S(2)}, u32[]{:S(2)}) async-start(f32[8,64,128]{2,1,0:T(8,128)} %get-tuple-element.5), calls=%async_computation | async-start | bytes 524288 | tf_op jit(solution)/shard_map/all_to_all | solution.py:256
  25.9 0.0 collective-permute-done.2.f2_ref
  26.0 0.0 collective-permute-done.3.f3_ref
  26.0 0.0 collective-permute-done.other_ref
  26.0 2.0 %in_grad_terms.1 = f32[8,64,128]{2,1,0:T(8,128)} custom-call(bf16[2,8,64,128]{3,2,1,0:T(8,128)(2,1)S(1)} %bitcast.8, bf16[2,8,64,128]{3,2,1,0:T(8,128)(2,1)S(1)} %collective-permute-done.other_ref, bf16[27,32,128]{2,1,0:T(8,128)(2,1)S(1)} %copy-done.2, bf16[27,32,128]{2,1,0:T(8,128)(2,1)S(1)} %collective-permute-done.1.f1_ref, ...), custom_call_target="tpu_custom_call" | custom-call | flops 452984832 | bytes 2000000 | tf_op jit(solution)/shard_map/in_grad_terms/pallas_call | solution.py:207
  27.9 4.5 %all-to-all-done = f32[8,64,128]{2,1,0:T(8,128)S(1)} async-done(((f32[8,64,128]{2,1,0:T(8,128)}), f32[8,64,128]{2,1,0:T(8,128)S(1)}, u32[]{:S(2)}, u32[]{:S(2)}) %all-to-all-start) | async-done | bytes 262176 | tf_op jit(solution)/shard_map/all_to_all | solution.py:256
  32.4 9.7 %all-to-all-start.2 = ((f32[8,64,128]{2,1,0:T(8,128)}), f32[8,64,128]{2,1,0:T(8,128)S(1)}, u32[]{:S(2)}, u32[]{:S(2)}) async-start(f32[8,64,128]{2,1,0:T(8,128)} %in_grad_terms.1), calls=%async_computation.2 | async-start | bytes 524288 | tf_op jit(solution)/shard_map/all_to_all | solution.py:254
  42.2 0.1 copy.7
  42.3 0.7 %convert_element_type.21 = bf16[32,256]{1,0:T(8,128)(2,1)} reshape(bf16[32,4,64]{2,1,0:T(4,128)(2,1)S(1)} %copy.8) | data formatting | bytes 32768 | tf_op jit(solution)/shard_map/convert_element_type | solution.py:258
  43.1 2.7 %filter_terms.1 = f32[27,32,128]{2,1,0:T(8,128)} custom-call(bf16[2,8,64,128]{3,2,1,0:T(8,128)(2,1)S(1)} %bitcast.9, bf16[1024,512]{1,0:T(8,128)(2,1)S(1)} %get-tuple-element.6.refs_1_), custom_call_target="tpu_custom_call" | custom-call | flops 452984832 | bytes 2000000 | tf_op jit(solution)/shard_map/filter_terms/pallas_call | solution.py:220
  45.7 7.7 %all-to-all-done.2 = f32[8,64,128]{2,1,0:T(8,128)S(1)} async-done(((f32[8,64,128]{2,1,0:T(8,128)}), f32[8,64,128]{2,1,0:T(8,128)S(1)}, u32[]{:S(2)}, u32[]{:S(2)}) %all-to-all-start.2) | async-done | bytes 262176 | tf_op jit(solution)/shard_map/all_to_all | solution.py:254
  53.4 0.6 %reduce_sum.19 = bf16[64,128]{1,0:T(8,128)(2,1)} reduce(f32[8,64,128]{2,1,0:T(8,128)S(1)} %all-to-all-done.2, f32[]{:T(128)} %constant.0.clone.1), dimensions={0}, to_apply=%region_1.0 | reduce | flops 57344 | bytes 278532 | tf_op jit(solution)/shard_map/reduce_sum | solution.py:255
  (2 shorter events, 0.0 us)
Async XLA Ops:
  0.6 0.7 %copy-start = (bf16[32,256]{1,0:T(8,128)(2,1)S(1)}, bf16[32,256]{1,0:T(8,128)(2,1)}, u32[]{:S(2)}) copy-start(bf16[32,256]{1,0:T(8,128)(2,1)} %grad_ref.1) | copy-start | bytes 49156
  1.3 16.6 %copy-start.1 = (bf16[128,2048]{1,0:T(8,128)(2,1)S(1)}, bf16[128,2048]{1,0:T(8,128)(2,1)}, u32[]{:S(2)}) copy-start(bf16[128,2048]{1,0:T(8,128)(2,1)} %x_ref.1) | copy-start | bytes 1572868
  2.2 7.3 %copy-start.2 = (bf16[27,32,128]{2,1,0:T(8,128)(2,1)S(1)}, bf16[27,32,128]{2,1,0:T(8,128)(2,1)}, u32[]{:S(2)}) copy-start(bf16[27,32,128]{2,1,0:T(8,128)(2,1)} %f0_ref.1) | copy-start | bytes 663556
  2.2 15.0 %all-to-all-start.1 = ((bf16[16,64,128]{2,1,0:T(8,128)(2,1)}), bf16[16,64,128]{2,1,0:T(8,128)(2,1)S(1)}, u32[]{:S(2)}, u32[]{:S(2)}) async-start(bf16[16,64,128]{2,1,0:T(8,128)(2,1)} %pack.1), calls=%async_computation.1 | async-start | bytes 524288 | tf_op jit(solution)/shard_map/all_to_all | solution.py:246
  9.5 8.4 %collective-permute-start.1 = (bf16[27,32,128]{2,1,0:T(8,128)(2,1)S(1)}, bf16[27,32,128]{2,1,0:T(8,128)(2,1)S(1)}, u32[]{:S(2)}, u32[]{:S(2)}) collective-permute-start(bf16[27,32,128]{2,1,0:T(8,128)(2,1)S(1)} %copy-done.2), channel_id=1, source_target_pairs={{0,16},{8,24},{16,0},{24,8},{32,48},{40,56},{48,32},{56,40},{64,80... | collective-permute-start | bytes 663560 | tf_op jit(solution)/shard_map/ppermute | solution.py:248
  17.2 8.7 %collective-permute-start = (bf16[2,8,64,128]{3,2,1,0:T(8,128)(2,1)S(1)}, bf16[2,8,64,128]{3,2,1,0:T(8,128)(2,1)S(1)}, u32[]{:S(2)}, u32[]{:S(2)}) collective-permute-start(bf16[2,8,64,128]{3,2,1,0:T(8,128)(2,1)S(1)} %bitcast.7), channel_id=1, source_target_pairs={{0,8},{8,0},{16,24},{24,16},{32,40},{40,32},{48,56},{56,48},{64,72... | collective-permute-start | bytes 786440 | tf_op jit(solution)/shard_map/ppermute | solution.py:252
  17.2 8.7 %collective-permute-start.2 = (bf16[27,32,128]{2,1,0:T(8,128)(2,1)S(1)}, bf16[27,32,128]{2,1,0:T(8,128)(2,1)S(1)}, u32[]{:S(2)}, u32[]{:S(2)}) collective-permute-start(bf16[27,32,128]{2,1,0:T(8,128)(2,1)S(1)} %copy-done.2), channel_id=1, source_target_pairs={{0,8},{8,0},{16,24},{24,16},{32,40},{40,32},{48,56},{56,48},{64,72... | collective-permute-start | bytes 663560 | tf_op jit(solution)/shard_map/ppermute | solution.py:249
  17.9 8.0 %collective-permute-start.3 = (bf16[27,32,128]{2,1,0:T(8,128)(2,1)S(1)}, bf16[27,32,128]{2,1,0:T(8,128)(2,1)S(1)}, u32[]{:S(2)}, u32[]{:S(2)}) collective-permute-start(bf16[27,32,128]{2,1,0:T(8,128)(2,1)S(1)} %collective-permute-done.1.f1_ref), channel_id=1, source_target_pairs={{0,8},{8,0},{16,24},{24,16},{32,40},{40,32},{48,56},{56,48},{64,72... | collective-permute-start | bytes 663560 | tf_op jit(solution)/shard_map/ppermute | solution.py:250
  20.2 12.2 %all-to-all-start = ((f32[8,64,128]{2,1,0:T(8,128)}), f32[8,64,128]{2,1,0:T(8,128)S(1)}, u32[]{:S(2)}, u32[]{:S(2)}) async-start(f32[8,64,128]{2,1,0:T(8,128)} %get-tuple-element.5), calls=%async_computation | async-start | bytes 524288 | tf_op jit(solution)/shard_map/all_to_all | solution.py:256
  32.4 20.9 %all-to-all-start.2 = ((f32[8,64,128]{2,1,0:T(8,128)}), f32[8,64,128]{2,1,0:T(8,128)S(1)}, u32[]{:S(2)}, u32[]{:S(2)}) async-start(f32[8,64,128]{2,1,0:T(8,128)} %in_grad_terms.1), calls=%async_computation.2 | async-start | bytes 524288 | tf_op jit(solution)/shard_map/all_to_all | solution.py:254
where the time goes:
time: 54.4 us; the launch traced here: 54 us
  starting transfers between devices  24.8 us (46%)
  waiting for transfers between devices  18.5 us (34%)
  Pallas kernels  7.81 us (14%)
  local copies, waits for them, and re-layouts  1.56 us (3%)
  between operations  0.67 us (1%)
  other arithmetic  0.64 us (1%)
    all_to_all x1, starting transfers between devices, body(): lax.all_to_all(shares, 'co', 0, 0, tiled=True, axis_index_groups=sum_groups)  9.74 us
    all_to_all x1, waiting for transfers between devices, body(): lax.all_to_all(shares, 'co', 0, 0, tiled=True, axis_index_groups=sum_groups)  7.67 us
    all_to_all x1, starting transfers between devices, body(): lax.all_to_all(packed, ('co', 'ci'), 0, 0, tiled=True, axis_index_groups=...  7.26 us
    all_to_all x1, waiting for transfers between devices, body(): lax.all_to_all(packed, ('co', 'ci'), 0, 0, tiled=True, axis_index_groups=...  6.21 us
    all_to_all x1, starting transfers between devices, body(): lax.all_to_all(terms, ('co', 'ci'), 0, 0, tiled=True, axis_index_groups=r...  5.7 us
    all_to_all x1, waiting for transfers between devices, body(): lax.all_to_all(terms, ('co', 'ci'), 0, 0, tiled=True, axis_index_groups=r...  4.5 us
    pallas_call x1, Pallas kernels, filter_terms(): pl.pallas_call(lambda *refs: filter_grad_kernel(*refs, scale=scale), out_...  2.65 us
    pallas_call x1, Pallas kernels, response_terms(): pl.pallas_call(response_kernel, out_shape=(jax.ShapeDtypeStruct((groups,...  2.33 us
  transfers between devices with their start and end apart: 7, of which 4 were waited for; matrix products, arithmetic and copies ran while one was open for 2% of the time, Pallas kernels for 13%

commit v1 on v0

--- a/solution.py
+++ b/solution.py
@@ -41,7 +41,11 @@
 
 def position():
     co = lax.axis_index("co")
-    return lax.rem(co, 2), lax.rem(co // 2, 2)
+    return lax.rem(co, 2), co // (lax.axis_size("co") // 2)
+
+
+def receiver():
+    return lax.axis_index("ci")
 
 
 def pack_kernel(grad_ref, out_ref):
@@ -54,8 +58,8 @@
         out_ref[r] = packed
 
 
-def response_kernel(x_ref, f_ref, out_ref, wide_ref, lhs, rhs):
-    groups = out_ref.shape[0]
+def response_kernel(x_ref, f_ref, keep_ref, send_ref, wide_ref, lhs, rhs):
+    groups = 2 * keep_ref.shape[0]
     planes = 4 * groups
     rows = groups * AREA
     width = 4 * LANES
@@ -98,29 +102,58 @@
     low = parts[0][0] + pltpu.roll(parts[0][1], AREA, 1)
     high = pltpu.roll(parts[1][0], AREA, 1) + parts[1][1]
     total = jnp.where(lane < AREA, low, high)
-    core, _ = position()
-    for g in range(groups):
-        out_ref[lax.rem(g + core * (groups // 2), groups)] = total[g * AREA:(g + 1) * AREA]
+    mask = lax.bitwise_and(receiver(), groups // 2 - 1)
+    lower = receiver() < groups // 2
+    for g in range(groups // 2):
+        near = total[g * AREA:(g + 1) * AREA]
+        far = total[(g + groups // 2) * AREA:(g + groups // 2 + 1) * AREA]
+        at = lax.bitwise_xor(mask, g)
+        keep_ref[at] = jnp.where(lower, near, far)
+        send_ref[at] = jnp.where(lower, far, near)
+
+
+def add_kernel(mine_ref, other_ref, keep_ref, send_ref):
+    for p in range(mine_ref.shape[0]):
+        total = mine_ref[p] + other_ref[p]
+        if p % 2:
+            send_ref[p // 2] = total
+        else:
+            keep_ref[p // 2] = total
+
+
+def response_out_kernel(mine_ref, other_ref, out_ref):
+    total = mine_ref[0] + other_ref[0]
+    turned = jnp.concatenate([total, total], axis=0).T
+    lane = lax.broadcasted_iota(jnp.int32, (32, LANES), 1)
+    for t in range(2):
+        low = turned[t * 64:t * 64 + 32]
+        high = turned[t * 64 + 32:t * 64 + 64]
+        out_ref[:, t * LANES:(t + 1) * LANES] = jnp.where(lane < AREA, low, high).astype(BF16)
 
 
 def in_grad_kernel(mine_ref, other_ref, f0_ref, f1_ref, f2_ref, f3_ref, out_ref, lhs, rhs):
     groups = out_ref.shape[0]
-    core, zpar = position()
-    q = 2 * zpar + core
-    rows = groups * AREA
+    held = groups // 2
+    core, half = position()
     filters = (f0_ref, f1_ref, f2_ref, f3_ref)
-    lane = lax.broadcasted_iota(jnp.int32, (rows, LANES), 1)
-    own_lane = jnp.where(q == 0, jnp.where(lane >= 32, 1, 0), jnp.where(lane < 160 - 32 * q, 1, 0)) == 1
-    back = lax.rem(160 - 32 * q, LANES)
-    edge = jnp.zeros((AREA, LANES), F32)
+    lane = lax.broadcasted_iota(jnp.int32, (AREA, LANES), 1)
     for source in range(4):
         ref = mine_ref if source < 2 else other_ref
-        sel = lax.rem(zpar + core + source // 2 + source % 2, 2)
-        block = ref[sel].reshape(rows, LANES).astype(F32)
-        rolled = pltpu.roll(block, back, 1)
-        below = jnp.concatenate([edge, rolled[:-AREA]], axis=0)
-        above = jnp.concatenate([rolled[AREA:], edge], axis=0)
-        near = jnp.where(own_lane, rolled, jnp.where(q == 0, below, above))
+        sel = half if source % 2 == 0 else 1 - half
+        blocks = []
+        for m in range(-1, held + 1):
+            at = half * held + m
+            block = ref[sel, jnp.clip(at, 0, groups - 1)].astype(F32)
+            if m in (-1, held):
+                block = jnp.where(jnp.logical_and(at >= 0, at < groups), block, 0.0)
+            blocks.append(block)
+        early = [pltpu.roll(block, 32 * (1 - core), 1) for block in blocks[:-1]]
+        late = [pltpu.roll(block, LANES - 32 * (core + 1), 1) for block in blocks[1:]]
+        rows = []
+        for m in range(held):
+            rows.append(jnp.where(lane >= 32 * (1 - core), early[m + 1], early[m]))
+            rows.append(jnp.where(lane < LANES - 32 * (core + 1), late[m], late[m + 1]))
+        near = jnp.concatenate(rows, axis=0)
         for b in range(3):
             at = (b * 4 + source) * LANES
             lhs[:, at:at + LANES] = shift_rows(near, 1 - b, 0).astype(BF16)
@@ -130,15 +163,13 @@
                 rhs[at + 96:at + LANES, c * LANES:(c + 1) * LANES] = jnp.zeros((32, LANES), BF16)
     full = jnp.dot(lhs[...], rhs[...], preferred_element_type=F32)
     total = shift_rows(full[:, :LANES], 0, 1) + full[:, LANES:2 * LANES] + shift_rows(full[:, 2 * LANES:], 0, -1)
-    for k in range(groups):
-        out_ref[lax.rem(k + (groups // 4) * q, groups)] = total[k * AREA:(k + 1) * AREA]
+    out_ref[...] = total.reshape(out_ref.shape)
 
 
 def filter_grad_kernel(mine_ref, wide_ref, out_ref, *, scale):
     groups = mine_ref.shape[1]
     rows = groups * AREA
-    core, zpar = position()
-    block = mine_ref[lax.rem(zpar + core, 2)].astype(F32).reshape(rows, LANES)
+    block = mine_ref[position()[1]].astype(F32).reshape(rows, LANES)
     turned = jnp.concatenate([block[k * LANES:(k + 1) * LANES].T for k in range(rows // LANES)], axis=1)
     turned = jnp.concatenate([turned[:64], turned[64:]], axis=1)
     cells = turned.shape[1]
@@ -189,16 +220,40 @@
     return pl.pallas_call(
         response_kernel,
         out_shape=(
-            jax.ShapeDtypeStruct((groups, AREA, LANES), F32),
+            jax.ShapeDtypeStruct((groups // 2, AREA, LANES), F32),
+            jax.ShapeDtypeStruct((groups // 2, AREA, LANES), F32),
             jax.ShapeDtypeStruct((2 * rows, 4 * LANES), BF16),
         ),
         in_specs=in_vmem(2),
-        out_specs=tuple(in_vmem(2)),
+        out_specs=tuple(in_vmem(3)),
         scratch_shapes=[VMEM((2 * rows, 12 * LANES), BF16), VMEM((2 * LANES, 12 * LANES), BF16)],
         compiler_params=params(),
         cost_estimate=cost(2 * 27 * 32 * 128 * 2048, 2 * 10**6),
         name="response_terms",
     )(features, bank)
+
+
+def add_terms(mine, other):
+    part = jax.ShapeDtypeStruct((mine.shape[0] // 2, AREA, LANES), F32)
+    return pl.pallas_call(
+        add_kernel,
+        out_shape=(part, part),
+        in_specs=in_vmem(2),
+        out_specs=tuple(in_vmem(2)),
+        compiler_params=params(),
+        name="add_terms",
+    )(mine, other)
+
+
+def response_out(mine, other):
+    return pl.pallas_call(
+        response_out_kernel,
+        out_shape=jax.ShapeDtypeStruct((32, 4 * AREA), BF16),
+        in_specs=in_vmem(2),
+        out_specs=in_vmem(1)[0],
+        compiler_params=params(),
+        name="response_out",
+    )(mine, other)
 
 
 def in_grad_terms(mine, other, banks):
@@ -232,30 +287,29 @@
     cell_count = features.shape[1]
     n_ci = lax.axis_size("ci")
     n_co = lax.axis_size("co")
-    other_z = [(i, i ^ 2) for i in range(n_co)]
+    column = n_co // 2
+    other_y = [(i, (i + column) % n_co) for i in range(n_co)]
     other_core = [(i, i ^ 1) for i in range(n_co)]
-    gather_groups = [
-        [(4 * k + 2 * ((h + c) % 2) + c) * n_ci + i for h in range(2) for i in range(n_ci)]
-        for k in range(n_co // 4)
-        for c in range(2)
-    ]
-    quads = n_co // 4
-    sum_groups = [[4 * ((k - quads // 4 * q) % quads) + q for k in range(quads)] for q in range(4)]
-    response_groups = [[o * n_ci + (i - o % 2 * n_ci // 2) % n_ci for i in range(n_ci)] for o in range(n_co)]
+    gather_groups = [[(h * column + k) * n_ci + i for h in range(2) for i in range(n_ci)] for k in range(column)]
+    sum_groups = [[h * column + 2 * z + c for z in range(column // 2)] for h in range(2) for c in range(2)]
+    flips = [[(i, i ^ d) for i in range(n_ci)] for d in (n_ci // 2, 1, 2)]
     packed = pack(out_grad, 2 * n_ci)
     mine = lax.all_to_all(packed, ("co", "ci"), 0, 0, tiled=True, axis_index_groups=gather_groups)
     mine = mine.reshape(2, n_ci, AREA, LANES)
-    bank_z = lax.ppermute(bank, "co", other_z)
+    bank_y = lax.ppermute(bank, "co", other_y)
     bank_c = lax.ppermute(bank, "co", other_core)
-    bank_cz = lax.ppermute(bank_z, "co", other_core)
-    terms, wide = response_terms(features, bank)
+    bank_cy = lax.ppermute(bank_y, "co", other_core)
+    keep, send, wide = response_terms(features, bank)
+    came = lax.ppermute(send, "ci", flips[0])
+    keep, send = add_terms(keep, came)
+    came = lax.ppermute(send, "ci", flips[1])
+    keep, send = add_terms(keep, came)
+    came = lax.ppermute(send, "ci", flips[2])
+    response = response_out(keep, came)
     other = lax.ppermute(mine, "co", other_core)
-    shares = in_grad_terms(mine, other, (bank, bank_z, bank_c, bank_cz))
+    shares = in_grad_terms(mine, other, (bank, bank_y, bank_c, bank_cy))
     shares = lax.all_to_all(shares, "co", 0, 0, tiled=True, axis_index_groups=sum_groups)
     in_grad = jnp.sum(shares, axis=0).T.astype(BF16)
-    terms = lax.all_to_all(terms, ("co", "ci"), 0, 0, tiled=True, axis_index_groups=response_groups)
-    response = jnp.sum(terms, axis=0).reshape(AREA, 4, 32).transpose(2, 1, 0)
-    response = response.reshape(32, 4 * AREA).astype(BF16)
     filter_grad = filter_terms(mine, wide, float(cell_count) ** (-0.5))
     return (response, in_grad, filter_grad)
 

time: 54.4 us -> 53.7 us (0.987)
  the two profiles are of different devices: /device:TPU:8 before, /device:TPU:6 now
where the time goes in v1:
time: 53.7 us; the launch traced here: 53.4 us
  starting transfers between devices  23 us (43%)
  waiting for transfers between devices  20.6 us (38%)
  Pallas kernels  7.78 us (14%)
  local copies, waits for them, and re-layouts  0.72 us (1%)
  between operations  0.67 us (1%)
  other arithmetic  0.62 us (1%)
    all_to_all x1, starting transfers between devices, body(): lax.all_to_all(shares, 'co', 0, 0, tiled=True, axis_index_groups=sum_groups)  8.46 us
    all_to_all x1, starting transfers between devices, body(): lax.all_to_all(packed, ('co', 'ci'), 0, 0, tiled=True, axis_index_groups=...  7.55 us
    ppermute x1, waiting for transfers between devices, body(): came = lax.ppermute(send, 'ci', flips[0])  4.33 us
    ppermute x1, waiting for transfers between devices, body(): came = lax.ppermute(send, 'ci', flips[2])  4.02 us
    ppermute x1, waiting for transfers between devices, body(): bank_y = lax.ppermute(bank, 'co', other_y)  3.68 us
    all_to_all x1, waiting for transfers between devices, body(): lax.all_to_all(packed, ('co', 'ci'), 0, 0, tiled=True, axis_index_groups=...  3.58 us
    ppermute x1, waiting for transfers between devices, body(): came = lax.ppermute(send, 'ci', flips[1])  3.47 us
    ppermute x1, starting transfers between devices, body(): bank_y = lax.ppermute(bank, 'co', other_y)  3.06 us
  transfers between devices with their start and end apart: 9, of which 6 were waited for; matrix products, arithmetic and copies ran while one was open for 0% of the time, Pallas kernels for 9%

profile of v1, /device:TPU:6, one launch (start us, length us, event | category | flops | bytes accessed | tf_op | source)
XLA Modules:
  0.0 53.4 jit_solution(2734601683251884973)
XLA Ops:
  0.6 0.0 copy-start
  0.6 0.7 %copy-done = bf16[32,256]{1,0:T(8,128)(2,1)S(1)} copy-done((bf16[32,256]{1,0:T(8,128)(2,1)S(1)}, bf16[32,256]{1,0:T(8,128)(2,1)}, u32[]{:S(2)}) %copy-start) | copy-done | bytes 16408
  1.3 0.9 %pack.1 = bf16[16,64,128]{2,1,0:T(8,128)(2,1)} custom-call(bf16[32,256]{1,0:T(8,128)(2,1)S(1)} %copy-done), custom_call_target="tpu_custom_call" | custom-call | tf_op jit(solution)/shard_map/pack/pallas_call | solution.py:207
  2.2 0.0 copy-start.2
  2.2 7.6 %all-to-all-start = ((bf16[16,64,128]{2,1,0:T(8,128)(2,1)}), bf16[16,64,128]{2,1,0:T(8,128)(2,1)S(1)}, u32[]{:S(2)}, u32[]{:S(2)}) async-start(bf16[16,64,128]{2,1,0:T(8,128)(2,1)} %pack.1), calls=%async_computation | async-start | bytes 524288 | tf_op jit(solution)/shard_map/all_to_all | solution.py:297
  9.8 0.0 copy-done.2
  9.8 3.1 %collective-permute-start.4 = (bf16[27,32,128]{2,1,0:T(8,128)(2,1)S(1)}, bf16[27,32,128]{2,1,0:T(8,128)(2,1)S(1)}, u32[]{:S(2)}, u32[]{:S(2)}) collective-permute-start(bf16[27,32,128]{2,1,0:T(8,128)(2,1)S(1)} %copy-done.2), channel_id=1, source_target_pairs={{0,128},{8,136},{16,144},{24,152},{32,160},{40,168},{48,176},{56,1... | collective-permute-start | bytes 663560 | tf_op jit(solution)/shard_map/ppermute | solution.py:299
  12.8 3.6 %all-to-all-done = bf16[16,64,128]{2,1,0:T(8,128)(2,1)S(1)} async-done(((bf16[16,64,128]{2,1,0:T(8,128)(2,1)}), bf16[16,64,128]{2,1,0:T(8,128)(2,1)S(1)}, u32[]{:S(2)}, u32[]{:S(2)}) %all-to-all-start) | async-done | bytes 262176 | tf_op jit(solution)/shard_map/all_to_all | solution.py:297
  16.4 0.0 copy-start.1
  16.4 0.0 collective-permute-start.3
  16.4 0.5 collective-permute-start.5
  16.9 3.7 %collective-permute-done.4.f1_ref = bf16[27,32,128]{2,1,0:T(8,128)(2,1)S(1)} collective-permute-done((bf16[27,32,128]{2,1,0:T(8,128)(2,1)S(1)}, bf16[27,32,128]{2,1,0:T(8,128)(2,1)S(1)}, u32[]{:S(2)}, u32[]{:S(2)}) %collective-permute-start.4) | collective-permute-done | bytes 221216 | tf_op jit(solution)/shard_map/ppermute | solution.py:299
  20.6 0.0 collective-permute-start.6
  20.6 0.0 collective-permute-done.5.f2_ref
  20.6 1.5 %collective-permute-done.6.f3_ref = bf16[27,32,128]{2,1,0:T(8,128)(2,1)S(1)} collective-permute-done((bf16[27,32,128]{2,1,0:T(8,128)(2,1)S(1)}, bf16[27,32,128]{2,1,0:T(8,128)(2,1)S(1)}, u32[]{:S(2)}, u32[]{:S(2)}) %collective-permute-start.6) | collective-permute-done | bytes 221216 | tf_op jit(solution)/shard_map/ppermute | solution.py:301
  22.1 0.0 collective-permute-done.3.other_ref
  22.1 1.9 %in_grad_terms.1 = f32[8,64,128]{2,1,0:T(8,128)} custom-call(bf16[2,8,64,128]{3,2,1,0:T(8,128)(2,1)S(1)} %bitcast.5, bf16[2,8,64,128]{3,2,1,0:T(8,128)(2,1)S(1)} %collective-permute-done.3.other_ref, bf16[27,32,128]{2,1,0:T(8,128)(2,1)S(1)} %copy-done.2, bf16[27,32,128]{2,1,0:T(8,128)(2,1)S(1)} %collective-permute-done.4.f1_ref, ...), custom_call_target="tpu_custom_call" | custom-call | flops 452984832 | bytes 2000000 | tf_op jit(solution)/shard_map/in_grad_terms/pallas_call | solution.py:262
  24.0 8.5 %all-to-all-start.1 = ((f32[8,64,128]{2,1,0:T(8,128)}), f32[8,64,128]{2,1,0:T(8,128)S(1)}, u32[]{:S(2)}, u32[]{:S(2)}) async-start(f32[8,64,128]{2,1,0:T(8,128)} %in_grad_terms.1), calls=%async_computation.1 | async-start | bytes 524288 | tf_op jit(solution)/shard_map/all_to_all | solution.py:311
  32.5 0.0 copy-done.1
  32.5 1.6 %response_terms.1 = (f32[4,64,128]{2,1,0:T(8,128)S(1)}, f32[4,64,128]{2,1,0:T(8,128)S(1)}, bf16[1024,512]{1,0:T(8,128)(2,1)S(1)}) custom-call(bf16[128,2048]{1,0:T(8,128)(2,1)S(1)} %copy-done.1, bf16[27,32,128]{2,1,0:T(8,128)(2,1)S(1)} %copy-done.2), custom_call_target="tpu_custom_call" | custom-call | flops 452984832 | bytes 2000000 | tf_op jit(solution)/shard_map/response_terms/pallas_call | solution.py:220
  34.1 1.0 %collective-permute-start = (f32[4,64,128]{2,1,0:T(8,128)S(1)}, f32[4,64,128]{2,1,0:T(8,128)S(1)}, u32[]{:S(2)}, u32[]{:S(2)}) collective-permute-start(f32[4,64,128]{2,1,0:T(8,128)S(1)} %get-tuple-element.11), channel_id=1, source_target_pairs={{0,4},{1,5},{2,6},{3,7},{4,0},{5,1},{6,2},{7,3},{8,12},{9,13},{10,... | collective-permute-start | bytes 393224 | tf_op jit(solution)/shard_map/ppermute | solution.py:303
  35.1 4.3 %collective-permute-done.other_ref = f32[4,64,128]{2,1,0:T(8,128)S(1)} collective-permute-done((f32[4,64,128]{2,1,0:T(8,128)S(1)}, f32[4,64,128]{2,1,0:T(8,128)S(1)}, u32[]{:S(2)}, u32[]{:S(2)}) %collective-permute-start) | collective-permute-done | bytes 131104 | tf_op jit(solution)/shard_map/ppermute | solution.py:303
  39.5 0.9 %collective-permute-start.1 = (f32[2,64,128]{2,1,0:T(8,128)S(1)}, f32[2,64,128]{2,1,0:T(8,128)S(1)}, u32[]{:S(2)}, u32[]{:S(2)}) collective-permute-start(f32[2,64,128]{2,1,0:T(8,128)S(1)} %get-tuple-element.13), channel_id=1, source_target_pairs={{0,1},{1,0},{2,3},{3,2},{4,5},{5,4},{6,7},{7,6},{8,9},{9,8},{10,11... | collective-permute-start | bytes 196616 | tf_op jit(solution)/shard_map/ppermute | solution.py:305
  40.4 3.5 %collective-permute-done.1.other_ref = f32[2,64,128]{2,1,0:T(8,128)S(1)} collective-permute-done((f32[2,64,128]{2,1,0:T(8,128)S(1)}, f32[2,64,128]{2,1,0:T(8,128)S(1)}, u32[]{:S(2)}, u32[]{:S(2)}) %collective-permute-start.1) | collective-permute-done | bytes 65568 | tf_op jit(solution)/shard_map/ppermute | solution.py:305
  43.9 1.5 %collective-permute-start.2 = (f32[1,64,128]{2,1,0:T(8,128)S(1)}, f32[1,64,128]{2,1,0:T(8,128)S(1)}, u32[]{:S(2)}, u32[]{:S(2)}) collective-permute-start(f32[1,64,128]{2,1,0:T(8,128)S(1)} %get-tuple-element.15), channel_id=1, source_target_pairs={{0,2},{1,3},{2,0},{3,1},{4,6},{5,7},{6,4},{7,5},{8,10},{9,11},{10,... | collective-permute-start | bytes 98312 | tf_op jit(solution)/shard_map/ppermute | solution.py:307
  45.4 4.0 %collective-permute-done.2.other_ref = f32[1,64,128]{2,1,0:T(8,128)S(1)} collective-permute-done((f32[1,64,128]{2,1,0:T(8,128)S(1)}, f32[1,64,128]{2,1,0:T(8,128)S(1)}, u32[]{:S(2)}, u32[]{:S(2)}) %collective-permute-start.2) | collective-permute-done | bytes 32800 | tf_op jit(solution)/shard_map/ppermute | solution.py:307
  49.4 0.7 %response_out.1 = bf16[32,256]{1,0:T(8,128)(2,1)} custom-call(f32[1,64,128]{2,1,0:T(8,128)S(1)} %get-tuple-element.14.mine_ref, f32[1,64,128]{2,1,0:T(8,128)S(1)} %collective-permute-done.2.other_ref), custom_call_target="tpu_custom_call" | custom-call | tf_op jit(solution)/shard_map/response_out/pallas_call | solution.py:249
  50.1 2.6 %filter_terms.1 = f32[27,32,128]{2,1,0:T(8,128)} custom-call(bf16[2,8,64,128]{3,2,1,0:T(8,128)(2,1)S(1)} %bitcast.6, bf16[1024,512]{1,0:T(8,128)(2,1)S(1)} %get-tuple-element.16.refs_1_), custom_call_target="tpu_custom_call" | custom-call | flops 452984832 | bytes 2000000 | tf_op jit(solution)/shard_map/filter_terms/pallas_call | solution.py:275
  52.8 0.0 all-to-all-done.1
  52.8 0.6 %reduce_sum.9 = bf16[64,128]{1,0:T(8,128)(2,1)} reduce(f32[8,64,128]{2,1,0:T(8,128)S(1)} %all-to-all-done.1, f32[]{:T(128)} %constant.0.clone.1), dimensions={0}, to_apply=%region_0.0 | reduce | flops 57344 | bytes 278532 | tf_op jit(solution)/shard_map/reduce_sum | solution.py:312
  (2 shorter events, 0.0 us)
Async XLA Ops:
  0.6 0.7 %copy-start = (bf16[32,256]{1,0:T(8,128)(2,1)S(1)}, bf16[32,256]{1,0:T(8,128)(2,1)}, u32[]{:S(2)}) copy-start(bf16[32,256]{1,0:T(8,128)(2,1)} %grad_ref.1) | copy-start | bytes 49156
  2.2 7.6 %copy-start.2 = (bf16[27,32,128]{2,1,0:T(8,128)(2,1)S(1)}, bf16[27,32,128]{2,1,0:T(8,128)(2,1)}, u32[]{:S(2)}) copy-start(bf16[27,32,128]{2,1,0:T(8,128)(2,1)} %f0_ref.1) | copy-start | bytes 663556
  2.2 14.2 %all-to-all-start = ((bf16[16,64,128]{2,1,0:T(8,128)(2,1)}), bf16[16,64,128]{2,1,0:T(8,128)(2,1)S(1)}, u32[]{:S(2)}, u32[]{:S(2)}) async-start(bf16[16,64,128]{2,1,0:T(8,128)(2,1)} %pack.1), calls=%async_computation | async-start | bytes 524288 | tf_op jit(solution)/shard_map/all_to_all | solution.py:297
  9.8 10.8 %collective-permute-start.4 = (bf16[27,32,128]{2,1,0:T(8,128)(2,1)S(1)}, bf16[27,32,128]{2,1,0:T(8,128)(2,1)S(1)}, u32[]{:S(2)}, u32[]{:S(2)}) collective-permute-start(bf16[27,32,128]{2,1,0:T(8,128)(2,1)S(1)} %copy-done.2), channel_id=1, source_target_pairs={{0,128},{8,136},{16,144},{24,152},{32,160},{40,168},{48,176},{56,1... | collective-permute-start | bytes 663560 | tf_op jit(solution)/shard_map/ppermute | solution.py:299
  16.4 16.1 %copy-start.1 = (bf16[128,2048]{1,0:T(8,128)(2,1)S(1)}, bf16[128,2048]{1,0:T(8,128)(2,1)}, u32[]{:S(2)}) copy-start(bf16[128,2048]{1,0:T(8,128)(2,1)} %x_ref.1) | copy-start | bytes 1572868
  16.4 5.7 %collective-permute-start.3 = (bf16[2,8,64,128]{3,2,1,0:T(8,128)(2,1)S(1)}, bf16[2,8,64,128]{3,2,1,0:T(8,128)(2,1)S(1)}, u32[]{:S(2)}, u32[]{:S(2)}) collective-permute-start(bf16[2,8,64,128]{3,2,1,0:T(8,128)(2,1)S(1)} %bitcast.4), channel_id=1, source_target_pairs={{0,8},{8,0},{16,24},{24,16},{32,40},{40,32},{48,56},{56,48},{64,72... | collective-permute-start | bytes 786440 | tf_op jit(solution)/shard_map/ppermute | solution.py:309
  16.4 4.2 %collective-permute-start.5 = (bf16[27,32,128]{2,1,0:T(8,128)(2,1)S(1)}, bf16[27,32,128]{2,1,0:T(8,128)(2,1)S(1)}, u32[]{:S(2)}, u32[]{:S(2)}) collective-permute-start(bf16[27,32,128]{2,1,0:T(8,128)(2,1)S(1)} %copy-done.2), channel_id=1, source_target_pairs={{0,8},{8,0},{16,24},{24,16},{32,40},{40,32},{48,56},{56,48},{64,72... | collective-permute-start | bytes 663560 | tf_op jit(solution)/shard_map/ppermute | solution.py:300
  20.6 1.5 %collective-permute-start.6 = (bf16[27,32,128]{2,1,0:T(8,128)(2,1)S(1)}, bf16[27,32,128]{2,1,0:T(8,128)(2,1)S(1)}, u32[]{:S(2)}, u32[]{:S(2)}) collective-permute-start(bf16[27,32,128]{2,1,0:T(8,128)(2,1)S(1)} %collective-permute-done.4.f1_ref), channel_id=1, source_target_pairs={{0,8},{8,0},{16,24},{24,16},{32,40},{40,32},{48,56},{56,48},{64,72... | collective-permute-start | bytes 663560 | tf_op jit(solution)/shard_map/ppermute | solution.py:301
  24.0 28.8 %all-to-all-start.1 = ((f32[8,64,128]{2,1,0:T(8,128)}), f32[8,64,128]{2,1,0:T(8,128)S(1)}, u32[]{:S(2)}, u32[]{:S(2)}) async-start(f32[8,64,128]{2,1,0:T(8,128)} %in_grad_terms.1), calls=%async_computation.1 | async-start | bytes 524288 | tf_op jit(solution)/shard_map/all_to_all | solution.py:311
  34.1 5.3 %collective-permute-start = (f32[4,64,128]{2,1,0:T(8,128)S(1)}, f32[4,64,128]{2,1,0:T(8,128)S(1)}, u32[]{:S(2)}, u32[]{:S(2)}) collective-permute-start(f32[4,64,128]{2,1,0:T(8,128)S(1)} %get-tuple-element.11), channel_id=1, source_target_pairs={{0,4},{1,5},{2,6},{3,7},{4,0},{5,1},{6,2},{7,3},{8,12},{9,13},{10,... | collective-permute-start | bytes 393224 | tf_op jit(solution)/shard_map/ppermute | solution.py:303
  39.5 4.4 %collective-permute-start.1 = (f32[2,64,128]{2,1,0:T(8,128)S(1)}, f32[2,64,128]{2,1,0:T(8,128)S(1)}, u32[]{:S(2)}, u32[]{:S(2)}) collective-permute-start(f32[2,64,128]{2,1,0:T(8,128)S(1)} %get-tuple-element.13), channel_id=1, source_target_pairs={{0,1},{1,0},{2,3},{3,2},{4,5},{5,4},{6,7},{7,6},{8,9},{9,8},{10,11... | collective-permute-start | bytes 196616 | tf_op jit(solution)/shard_map/ppermute | solution.py:305
  43.9 5.5 %collective-permute-start.2 = (f32[1,64,128]{2,1,0:T(8,128)S(1)}, f32[1,64,128]{2,1,0:T(8,128)S(1)}, u32[]{:S(2)}, u32[]{:S(2)}) collective-permute-start(f32[1,64,128]{2,1,0:T(8,128)S(1)} %get-tuple-element.15), channel_id=1, source_target_pairs={{0,2},{1,3},{2,0},{3,1},{4,6},{5,7},{6,4},{7,5},{8,10},{9,11},{10,... | collective-permute-start | bytes 98312 | tf_op jit(solution)/shard_map/ppermute | solution.py:307

commit v2 on v1

--- a/solution.py
+++ b/solution.py
@@ -15,6 +15,9 @@
 
 
 VMEM = pltpu.VMEM
+H_FLIP = 0
+CI_FLIP = 7
+Z_ORDER = (7, 6, 5, 4, 3, 2, 1, 0)
 SHIFTS = [(b, c) for b in (-1, 0, 1) for c in (-1, 0, 1)]
 
 
@@ -42,6 +45,10 @@
 def position():
     co = lax.axis_index("co")
     return lax.rem(co, 2), co // (lax.axis_size("co") // 2)
+
+
+def flip(index, mask):
+    return lax.bitwise_xor(index, mask)
 
 
 def receiver():
@@ -143,7 +150,7 @@
         blocks = []
         for m in range(-1, held + 1):
             at = half * held + m
-            block = ref[sel, jnp.clip(at, 0, groups - 1)].astype(F32)
+            block = ref[flip(sel, H_FLIP), flip(jnp.clip(at, 0, groups - 1), CI_FLIP)].astype(F32)
             if m in (-1, held):
                 block = jnp.where(jnp.logical_and(at >= 0, at < groups), block, 0.0)
             blocks.append(block)
@@ -163,14 +170,16 @@
                 rhs[at + 96:at + LANES, c * LANES:(c + 1) * LANES] = jnp.zeros((32, LANES), BF16)
     full = jnp.dot(lhs[...], rhs[...], preferred_element_type=F32)
     total = shift_rows(full[:, :LANES], 0, 1) + full[:, LANES:2 * LANES] + shift_rows(full[:, 2 * LANES:], 0, -1)
-    out_ref[...] = total.reshape(out_ref.shape)
+    for k, z in enumerate(Z_ORDER):
+        out_ref[k] = total[z * AREA:(z + 1) * AREA]
 
 
 def filter_grad_kernel(mine_ref, wide_ref, out_ref, *, scale):
     groups = mine_ref.shape[1]
     rows = groups * AREA
-    block = mine_ref[position()[1]].astype(F32).reshape(rows, LANES)
-    turned = jnp.concatenate([block[k * LANES:(k + 1) * LANES].T for k in range(rows // LANES)], axis=1)
+    half = flip(position()[1], H_FLIP)
+    cells = jnp.concatenate([mine_ref[half, k ^ CI_FLIP].astype(F32) for k in range(groups)], axis=0)
+    turned = jnp.concatenate([cells[k * LANES:(k + 1) * LANES].T for k in range(rows // LANES)], axis=1)
     turned = jnp.concatenate([turned[:64], turned[64:]], axis=1)
     cells = turned.shape[1]
     index = lax.broadcasted_iota(jnp.int32, turned.shape, 1)
@@ -290,8 +299,10 @@
     column = n_co // 2
     other_y = [(i, (i + column) % n_co) for i in range(n_co)]
     other_core = [(i, i ^ 1) for i in range(n_co)]
-    gather_groups = [[(h * column + k) * n_ci + i for h in range(2) for i in range(n_ci)] for k in range(column)]
-    sum_groups = [[h * column + 2 * z + c for z in range(column // 2)] for h in range(2) for c in range(2)]
+    gather_groups = [
+        [((h ^ H_FLIP) * column + k) * n_ci + (i ^ CI_FLIP) for h in range(2) for i in range(n_ci)] for k in range(column)
+    ]
+    sum_groups = [[h * column + 2 * z + c for z in Z_ORDER] for h in range(2) for c in range(2)]
     flips = [[(i, i ^ d) for i in range(n_ci)] for d in (n_ci // 2, 1, 2)]
     packed = pack(out_grad, 2 * n_ci)
     mine = lax.all_to_all(packed, ("co", "ci"), 0, 0, tiled=True, axis_index_groups=gather_groups)

time: 53.7 us -> 55.4 us (1.032)
  the two profiles are of different devices: /device:TPU:6 before, /device:TPU:32 now
where the time goes in v2:
time: 55.4 us; the launch traced here: 55 us
  waiting for transfers between devices  23 us (42%)
  starting transfers between devices  22.3 us (40%)
  Pallas kernels  7.79 us (14%)
  local copies, waits for them, and re-layouts  0.72 us (1%)
  between operations  0.67 us (1%)
  other arithmetic  0.62 us (1%)
    all_to_all x1, starting transfers between devices, body(): lax.all_to_all(shares, 'co', 0, 0, tiled=True, axis_index_groups=sum_groups)  8.75 us
    all_to_all x1, waiting for transfers between devices, body(): lax.all_to_all(packed, ('co', 'ci'), 0, 0, tiled=True, axis_index_groups=...  8.47 us
    all_to_all x1, starting transfers between devices, body(): lax.all_to_all(packed, ('co', 'ci'), 0, 0, tiled=True, axis_index_groups=...  8.33 us
    ppermute x1, waiting for transfers between devices, body(): came = lax.ppermute(send, 'ci', flips[0])  5.19 us
    ppermute x1, waiting for transfers between devices, body(): came = lax.ppermute(send, 'ci', flips[2])  3.93 us
    ppermute x1, waiting for transfers between devices, body(): came = lax.ppermute(send, 'ci', flips[1])  3.74 us
    pallas_call x1, Pallas kernels, filter_terms(): pl.pallas_call(lambda *refs: filter_grad_kernel(*refs, scale=scale), out_...  2.65 us
    ppermute x1, starting transfers between devices, body(): bank_y = lax.ppermute(bank, 'co', other_y)  2.16 us
  transfers between devices with their start and end apart: 9, of which 6 were waited for; matrix products, arithmetic and copies ran while one was open for 0% of the time, Pallas kernels for 9%

profile of v2, /device:TPU:32, one launch (start us, length us, event | category | flops | bytes accessed | tf_op | source)
XLA Modules:
  0.0 55.0 jit_solution(13605230690482801719)
XLA Ops:
  0.6 0.0 copy-start
  0.6 0.7 %copy-done = bf16[32,256]{1,0:T(8,128)(2,1)S(1)} copy-done((bf16[32,256]{1,0:T(8,128)(2,1)S(1)}, bf16[32,256]{1,0:T(8,128)(2,1)}, u32[]{:S(2)}) %copy-start) | copy-done | bytes 16408
  1.3 0.9 %pack.1 = bf16[16,64,128]{2,1,0:T(8,128)(2,1)} custom-call(bf16[32,256]{1,0:T(8,128)(2,1)S(1)} %copy-done), custom_call_target="tpu_custom_call" | custom-call | tf_op jit(solution)/shard_map/pack/pallas_call | solution.py:216
  2.2 0.0 copy-start.2
  2.2 8.3 %all-to-all-start = ((bf16[16,64,128]{2,1,0:T(8,128)(2,1)}), bf16[16,64,128]{2,1,0:T(8,128)(2,1)S(1)}, u32[]{:S(2)}, u32[]{:S(2)}) async-start(bf16[16,64,128]{2,1,0:T(8,128)(2,1)} %pack.1), calls=%async_computation | async-start | bytes 524288 | tf_op jit(solution)/shard_map/all_to_all | solution.py:308
  10.5 0.0 copy-done.2
  10.5 2.2 %collective-permute-start.4 = (bf16[27,32,128]{2,1,0:T(8,128)(2,1)S(1)}, bf16[27,32,128]{2,1,0:T(8,128)(2,1)S(1)}, u32[]{:S(2)}, u32[]{:S(2)}) collective-permute-start(bf16[27,32,128]{2,1,0:T(8,128)(2,1)S(1)} %copy-done.2), channel_id=1, source_target_pairs={{0,128},{8,136},{16,144},{24,152},{32,160},{40,168},{48,176},{56,1... | collective-permute-start | bytes 663560 | tf_op jit(solution)/shard_map/ppermute | solution.py:310
  12.7 8.5 %all-to-all-done = bf16[16,64,128]{2,1,0:T(8,128)(2,1)S(1)} async-done(((bf16[16,64,128]{2,1,0:T(8,128)(2,1)}), bf16[16,64,128]{2,1,0:T(8,128)(2,1)S(1)}, u32[]{:S(2)}, u32[]{:S(2)}) %all-to-all-start) | async-done | bytes 262176 | tf_op jit(solution)/shard_map/all_to_all | solution.py:308
  21.2 0.0 copy-start.1
  21.2 0.0 collective-permute-start.3
  21.2 0.5 collective-permute-start.5
  21.7 0.0 collective-permute-done.4.f1_ref
  21.7 0.0 collective-permute-start.6
  21.7 1.3 %collective-permute-done.5.f2_ref = bf16[27,32,128]{2,1,0:T(8,128)(2,1)S(1)} collective-permute-done((bf16[27,32,128]{2,1,0:T(8,128)(2,1)S(1)}, bf16[27,32,128]{2,1,0:T(8,128)(2,1)S(1)}, u32[]{:S(2)}, u32[]{:S(2)}) %collective-permute-start.5) | collective-permute-done | bytes 221216 | tf_op jit(solution)/shard_map/ppermute | solution.py:311
  23.0 0.3 collective-permute-done.6.f3_ref
  23.3 0.0 collective-permute-done.3.other_ref
  23.4 1.9 %in_grad_terms.1 = f32[8,64,128]{2,1,0:T(8,128)} custom-call(bf16[2,8,64,128]{3,2,1,0:T(8,128)(2,1)S(1)} %bitcast.5, bf16[2,8,64,128]{3,2,1,0:T(8,128)(2,1)S(1)} %collective-permute-done.3.other_ref, bf16[27,32,128]{2,1,0:T(8,128)(2,1)S(1)} %copy-done.2, bf16[27,32,128]{2,1,0:T(8,128)(2,1)S(1)} %collective-permute-done.4.f1_ref, ...), custom_call_target="tpu_custom_call" | custom-call | flops 452984832 | bytes 2000000 | tf_op jit(solution)/shard_map/in_grad_terms/pallas_call | solution.py:271
  25.3 8.7 %all-to-all-start.1 = ((f32[8,64,128]{2,1,0:T(8,128)}), f32[8,64,128]{2,1,0:T(8,128)S(1)}, u32[]{:S(2)}, u32[]{:S(2)}) async-start(f32[8,64,128]{2,1,0:T(8,128)} %in_grad_terms.1), calls=%async_computation.1 | async-start | bytes 524288 | tf_op jit(solution)/shard_map/all_to_all | solution.py:322
  34.0 0.0 copy-done.1
  34.0 1.6 %response_terms.1 = (f32[4,64,128]{2,1,0:T(8,128)S(1)}, f32[4,64,128]{2,1,0:T(8,128)S(1)}, bf16[1024,512]{1,0:T(8,128)(2,1)S(1)}) custom-call(bf16[128,2048]{1,0:T(8,128)(2,1)S(1)} %copy-done.1, bf16[27,32,128]{2,1,0:T(8,128)(2,1)S(1)} %copy-done.2), custom_call_target="tpu_custom_call" | custom-call | flops 452984832 | bytes 2000000 | tf_op jit(solution)/shard_map/response_terms/pallas_call | solution.py:229
  35.7 0.2 collective-permute-start
  35.8 5.2 %collective-permute-done.other_ref = f32[4,64,128]{2,1,0:T(8,128)S(1)} collective-permute-done((f32[4,64,128]{2,1,0:T(8,128)S(1)}, f32[4,64,128]{2,1,0:T(8,128)S(1)}, u32[]{:S(2)}, u32[]{:S(2)}) %collective-permute-start) | collective-permute-done | bytes 131104 | tf_op jit(solution)/shard_map/ppermute | solution.py:314
  41.0 0.8 %collective-permute-start.1 = (f32[2,64,128]{2,1,0:T(8,128)S(1)}, f32[2,64,128]{2,1,0:T(8,128)S(1)}, u32[]{:S(2)}, u32[]{:S(2)}) collective-permute-start(f32[2,64,128]{2,1,0:T(8,128)S(1)} %get-tuple-element.13), channel_id=1, source_target_pairs={{0,1},{1,0},{2,3},{3,2},{4,5},{5,4},{6,7},{7,6},{8,9},{9,8},{10,11... | collective-permute-start | bytes 196616 | tf_op jit(solution)/shard_map/ppermute | solution.py:316
  41.8 3.7 %collective-permute-done.1.other_ref = f32[2,64,128]{2,1,0:T(8,128)S(1)} collective-permute-done((f32[2,64,128]{2,1,0:T(8,128)S(1)}, f32[2,64,128]{2,1,0:T(8,128)S(1)}, u32[]{:S(2)}, u32[]{:S(2)}) %collective-permute-start.1) | collective-permute-done | bytes 65568 | tf_op jit(solution)/shard_map/ppermute | solution.py:316
  45.5 1.6 %collective-permute-start.2 = (f32[1,64,128]{2,1,0:T(8,128)S(1)}, f32[1,64,128]{2,1,0:T(8,128)S(1)}, u32[]{:S(2)}, u32[]{:S(2)}) collective-permute-start(f32[1,64,128]{2,1,0:T(8,128)S(1)} %get-tuple-element.15), channel_id=1, source_target_pairs={{0,2},{1,3},{2,0},{3,1},{4,6},{5,7},{6,4},{7,5},{8,10},{9,11},{10,... | collective-permute-start | bytes 98312 | tf_op jit(solution)/shard_map/ppermute | solution.py:318
  47.1 3.9 %collective-permute-done.2.other_ref = f32[1,64,128]{2,1,0:T(8,128)S(1)} collective-permute-done((f32[1,64,128]{2,1,0:T(8,128)S(1)}, f32[1,64,128]{2,1,0:T(8,128)S(1)}, u32[]{:S(2)}, u32[]{:S(2)}) %collective-permute-start.2) | collective-permute-done | bytes 32800 | tf_op jit(solution)/shard_map/ppermute | solution.py:318
  51.1 0.7 %response_out.1 = bf16[32,256]{1,0:T(8,128)(2,1)} custom-call(f32[1,64,128]{2,1,0:T(8,128)S(1)} %get-tuple-element.14.mine_ref, f32[1,64,128]{2,1,0:T(8,128)S(1)} %collective-permute-done.2.other_ref), custom_call_target="tpu_custom_call" | custom-call | tf_op jit(solution)/shard_map/response_out/pallas_call | solution.py:258
  51.8 2.7 %filter_terms.1 = f32[27,32,128]{2,1,0:T(8,128)} custom-call(bf16[2,8,64,128]{3,2,1,0:T(8,128)(2,1)S(1)} %bitcast.6, bf16[1024,512]{1,0:T(8,128)(2,1)S(1)} %get-tuple-element.16.refs_1_), custom_call_target="tpu_custom_call" | custom-call | flops 452984832 | bytes 2000000 | tf_op jit(solution)/shard_map/filter_terms/pallas_call | solution.py:284
  54.4 0.0 all-to-all-done.1
  54.4 0.6 %reduce_sum.9 = bf16[64,128]{1,0:T(8,128)(2,1)} reduce(f32[8,64,128]{2,1,0:T(8,128)S(1)} %all-to-all-done.1, f32[]{:T(128)} %constant.0.clone.1), dimensions={0}, to_apply=%region_0.0 | reduce | flops 57344 | bytes 278532 | tf_op jit(solution)/shard_map/reduce_sum | solution.py:323
  (2 shorter events, 0.0 us)
Async XLA Ops:
  0.6 0.7 %copy-start = (bf16[32,256]{1,0:T(8,128)(2,1)S(1)}, bf16[32,256]{1,0:T(8,128)(2,1)}, u32[]{:S(2)}) copy-start(bf16[32,256]{1,0:T(8,128)(2,1)} %grad_ref.1) | copy-start | bytes 49156
  2.2 8.3 %copy-start.2 = (bf16[27,32,128]{2,1,0:T(8,128)(2,1)S(1)}, bf16[27,32,128]{2,1,0:T(8,128)(2,1)}, u32[]{:S(2)}) copy-start(bf16[27,32,128]{2,1,0:T(8,128)(2,1)} %f0_ref.1) | copy-start | bytes 663556
  2.2 19.0 %all-to-all-start = ((bf16[16,64,128]{2,1,0:T(8,128)(2,1)}), bf16[16,64,128]{2,1,0:T(8,128)(2,1)S(1)}, u32[]{:S(2)}, u32[]{:S(2)}) async-start(bf16[16,64,128]{2,1,0:T(8,128)(2,1)} %pack.1), calls=%async_computation | async-start | bytes 524288 | tf_op jit(solution)/shard_map/all_to_all | solution.py:308
  10.5 11.1 %collective-permute-start.4 = (bf16[27,32,128]{2,1,0:T(8,128)(2,1)S(1)}, bf16[27,32,128]{2,1,0:T(8,128)(2,1)S(1)}, u32[]{:S(2)}, u32[]{:S(2)}) collective-permute-start(bf16[27,32,128]{2,1,0:T(8,128)(2,1)S(1)} %copy-done.2), channel_id=1, source_target_pairs={{0,128},{8,136},{16,144},{24,152},{32,160},{40,168},{48,176},{56,1... | collective-permute-start | bytes 663560 | tf_op jit(solution)/shard_map/ppermute | solution.py:310
  21.2 12.8 %copy-start.1 = (bf16[128,2048]{1,0:T(8,128)(2,1)S(1)}, bf16[128,2048]{1,0:T(8,128)(2,1)}, u32[]{:S(2)}) copy-start(bf16[128,2048]{1,0:T(8,128)(2,1)} %x_ref.1) | copy-start | bytes 1572868
  21.2 2.2 %collective-permute-start.3 = (bf16[2,8,64,128]{3,2,1,0:T(8,128)(2,1)S(1)}, bf16[2,8,64,128]{3,2,1,0:T(8,128)(2,1)S(1)}, u32[]{:S(2)}, u32[]{:S(2)}) collective-permute-start(bf16[2,8,64,128]{3,2,1,0:T(8,128)(2,1)S(1)} %bitcast.4), channel_id=1, source_target_pairs={{0,8},{8,0},{16,24},{24,16},{32,40},{40,32},{48,56},{56,48},{64,72... | collective-permute-start | bytes 786440 | tf_op jit(solution)/shard_map/ppermute | solution.py:320
  21.2 1.8 %collective-permute-start.5 = (bf16[27,32,128]{2,1,0:T(8,128)(2,1)S(1)}, bf16[27,32,128]{2,1,0:T(8,128)(2,1)S(1)}, u32[]{:S(2)}, u32[]{:S(2)}) collective-permute-start(bf16[27,32,128]{2,1,0:T(8,128)(2,1)S(1)} %copy-done.2), channel_id=1, source_target_pairs={{0,8},{8,0},{16,24},{24,16},{32,40},{40,32},{48,56},{56,48},{64,72... | collective-permute-start | bytes 663560 | tf_op jit(solution)/shard_map/ppermute | solution.py:311
  21.7 1.7 %collective-permute-start.6 = (bf16[27,32,128]{2,1,0:T(8,128)(2,1)S(1)}, bf16[27,32,128]{2,1,0:T(8,128)(2,1)S(1)}, u32[]{:S(2)}, u32[]{:S(2)}) collective-permute-start(bf16[27,32,128]{2,1,0:T(8,128)(2,1)S(1)} %collective-permute-done.4.f1_ref), channel_id=1, source_target_pairs={{0,8},{8,0},{16,24},{24,16},{32,40},{40,32},{48,56},{56,48},{64,72... | collective-permute-start | bytes 663560 | tf_op jit(solution)/shard_map/ppermute | solution.py:312
  25.3 29.1 %all-to-all-start.1 = ((f32[8,64,128]{2,1,0:T(8,128)}), f32[8,64,128]{2,1,0:T(8,128)S(1)}, u32[]{:S(2)}, u32[]{:S(2)}) async-start(f32[8,64,128]{2,1,0:T(8,128)} %in_grad_terms.1), calls=%async_computation.1 | async-start | bytes 524288 | tf_op jit(solution)/shard_map/all_to_all | solution.py:322
  35.7 5.3 %collective-permute-start = (f32[4,64,128]{2,1,0:T(8,128)S(1)}, f32[4,64,128]{2,1,0:T(8,128)S(1)}, u32[]{:S(2)}, u32[]{:S(2)}) collective-permute-start(f32[4,64,128]{2,1,0:T(8,128)S(1)} %get-tuple-element.11), channel_id=1, source_target_pairs={{0,4},{1,5},{2,6},{3,7},{4,0},{5,1},{6,2},{7,3},{8,12},{9,13},{10,... | collective-permute-start | bytes 393224 | tf_op jit(solution)/shard_map/ppermute | solution.py:314
  41.0 4.5 %collective-permute-start.1 = (f32[2,64,128]{2,1,0:T(8,128)S(1)}, f32[2,64,128]{2,1,0:T(8,128)S(1)}, u32[]{:S(2)}, u32[]{:S(2)}) collective-permute-start(f32[2,64,128]{2,1,0:T(8,128)S(1)} %get-tuple-element.13), channel_id=1, source_target_pairs={{0,1},{1,0},{2,3},{3,2},{4,5},{5,4},{6,7},{7,6},{8,9},{9,8},{10,11... | collective-permute-start | bytes 196616 | tf_op jit(solution)/shard_map/ppermute | solution.py:316
  45.5 5.5 %collective-permute-start.2 = (f32[1,64,128]{2,1,0:T(8,128)S(1)}, f32[1,64,128]{2,1,0:T(8,128)S(1)}, u32[]{:S(2)}, u32[]{:S(2)}) collective-permute-start(f32[1,64,128]{2,1,0:T(8,128)S(1)} %get-tuple-element.15), channel_id=1, source_target_pairs={{0,2},{1,3},{2,0},{3,1},{4,6},{5,7},{6,4},{7,5},{8,10},{9,11},{10,... | collective-permute-start | bytes 98312 | tf_op jit(solution)/shard_map/ppermute | solution.py:318

commit v3 on v2

--- a/solution.py
+++ b/solution.py
@@ -17,7 +17,7 @@
 VMEM = pltpu.VMEM
 H_FLIP = 0
 CI_FLIP = 7
-Z_ORDER = (7, 6, 5, 4, 3, 2, 1, 0)
+Z_ORDER = (6, 5, 4, 3, 2, 1, 0, 7)
 SHIFTS = [(b, c) for b in (-1, 0, 1) for c in (-1, 0, 1)]
 
 
@@ -138,19 +138,18 @@
         out_ref[:, t * LANES:(t + 1) * LANES] = jnp.where(lane < AREA, low, high).astype(BF16)
 
 
-def in_grad_kernel(mine_ref, other_ref, f0_ref, f1_ref, f2_ref, f3_ref, out_ref, lhs, rhs):
+def in_grad_kernel(grad_ref, near_ref, far_ref, *rest):
+    *start, out_ref, lhs, rhs = rest
     groups = out_ref.shape[0]
     held = groups // 2
     core, half = position()
-    filters = (f0_ref, f1_ref, f2_ref, f3_ref)
     lane = lax.broadcasted_iota(jnp.int32, (AREA, LANES), 1)
-    for source in range(4):
-        ref = mine_ref if source < 2 else other_ref
-        sel = half if source % 2 == 0 else 1 - half
+    for source, bank_ref in enumerate((near_ref, far_ref)):
+        sel = half if source == 0 else 1 - half
         blocks = []
         for m in range(-1, held + 1):
             at = half * held + m
-            block = ref[flip(sel, H_FLIP), flip(jnp.clip(at, 0, groups - 1), CI_FLIP)].astype(F32)
+            block = grad_ref[flip(sel, H_FLIP), flip(jnp.clip(at, 0, groups - 1), CI_FLIP)].astype(F32)
             if m in (-1, held):
                 block = jnp.where(jnp.logical_and(at >= 0, at < groups), block, 0.0)
             blocks.append(block)
@@ -162,16 +161,17 @@
             rows.append(jnp.where(lane < LANES - 32 * (core + 1), late[m], late[m + 1]))
         near = jnp.concatenate(rows, axis=0)
         for b in range(3):
-            at = (b * 4 + source) * LANES
+            at = (b * 2 + source) * LANES
             lhs[:, at:at + LANES] = shift_rows(near, 1 - b, 0).astype(BF16)
             for c in range(3):
                 for j in range(3):
-                    rhs[at + j * 32:at + (j + 1) * 32, c * LANES:(c + 1) * LANES] = filters[source][(2 - j) * 9 + b * 3 + c]
+                    rhs[at + j * 32:at + (j + 1) * 32, c * LANES:(c + 1) * LANES] = bank_ref[(2 - j) * 9 + b * 3 + c]
                 rhs[at + 96:at + LANES, c * LANES:(c + 1) * LANES] = jnp.zeros((32, LANES), BF16)
     full = jnp.dot(lhs[...], rhs[...], preferred_element_type=F32)
     total = shift_rows(full[:, :LANES], 0, 1) + full[:, LANES:2 * LANES] + shift_rows(full[:, 2 * LANES:], 0, -1)
     for k, z in enumerate(Z_ORDER):
-        out_ref[k] = total[z * AREA:(z + 1) * AREA]
+        part = total[z * AREA:(z + 1) * AREA]
+        out_ref[k] = part + start[0][k] if start else part
 
 
 def filter_grad_kernel(mine_ref, wide_ref, out_ref, *, scale):
@@ -265,19 +265,19 @@
     )(mine, other)
 
 
-def in_grad_terms(mine, other, banks):
-    groups = mine.shape[1]
+def in_grad_terms(grads, banks, *start):
+    groups = grads.shape[1]
     rows = groups * AREA
     return pl.pallas_call(
         in_grad_kernel,
         out_shape=jax.ShapeDtypeStruct((groups, AREA, LANES), F32),
-        in_specs=in_vmem(6),
+        in_specs=in_vmem(3 + len(start)),
         out_specs=in_vmem(1)[0],
-        scratch_shapes=[VMEM((rows, 12 * LANES), BF16), VMEM((12 * LANES, 3 * LANES), BF16)],
-        compiler_params=params(),
-        cost_estimate=cost(2 * 27 * 32 * 128 * 2048, 2 * 10**6),
+        scratch_shapes=[VMEM((rows, 6 * LANES), BF16), VMEM((6 * LANES, 3 * LANES), BF16)],
+        compiler_params=params(),
+        cost_estimate=cost(27 * 32 * 128 * 2048, 10**6),
         name="in_grad_terms",
-    )(mine, other, *banks)
+    )(grads, *banks, *start)
 
 
 def filter_terms(mine, wide, scale):
@@ -318,7 +318,8 @@
     came = lax.ppermute(send, "ci", flips[2])
     response = response_out(keep, came)
     other = lax.ppermute(mine, "co", other_core)
-    shares = in_grad_terms(mine, other, (bank, bank_y, bank_c, bank_cy))
+    shares = in_grad_terms(mine, (bank, bank_y))
+    shares = in_grad_terms(other, (bank_c, bank_cy), shares)
     shares = lax.all_to_all(shares, "co", 0, 0, tiled=True, axis_index_groups=sum_groups)
     in_grad = jnp.sum(shares, axis=0).T.astype(BF16)
     filter_grad = filter_terms(mine, wide, float(cell_count) ** (-0.5))

time: 55.4 us -> 55.5 us (level)
  waiting for transfers between devices: 23 us -> 22.2 us
    ppermute x1, waiting for transfers between devices: 1.33 us -> 0.6 us  [body(): bank_c = lax.ppermute(bank, 'co', other_core)]
    all_to_all x1, starting transfers between devices: 8.75 us -> 9.31 us  [body(): lax.all_to_all(shares, 'co', 0, 0, tiled=True, axis_index_groups=sum_groups)]
    pallas_call x1 -> x2, Pallas kernels: 1.91 us -> 2.14 us  [in_grad_terms(): pl.pallas_call(in_grad_kernel, out_shape=jax.ShapeDtypeStruct((groups, AR...]
  transfers between devices with their start and end apart: 9 -> 9, of which waited for: 6 -> 6; matrix products, arithmetic and copies ran while one was open for 0% -> 0% of each run, Pallas kernels for 9% -> 10%
where the time goes in v3:
time: 55.5 us; the launch traced here: 55.1 us
  starting transfers between devices  22.8 us (41%)
  waiting for transfers between devices  22.2 us (40%)
  Pallas kernels  8.02 us (14%)
  local copies, waits for them, and re-layouts  0.72 us (1%)
  between operations  0.68 us (1%)
  other arithmetic  0.62 us (1%)
    all_to_all x1, starting transfers between devices, body(): lax.all_to_all(shares, 'co', 0, 0, tiled=True, axis_index_groups=sum_groups)  9.31 us
    all_to_all x1, waiting for transfers between devices, body(): lax.all_to_all(packed, ('co', 'ci'), 0, 0, tiled=True, axis_index_groups=...  8.47 us
    all_to_all x1, starting transfers between devices, body(): lax.all_to_all(packed, ('co', 'ci'), 0, 0, tiled=True, axis_index_groups=...  8.33 us
    ppermute x1, waiting for transfers between devices, body(): came = lax.ppermute(send, 'ci', flips[0])  5.18 us
    ppermute x1, waiting for transfers between devices, body(): came = lax.ppermute(send, 'ci', flips[2])  3.93 us
    ppermute x1, waiting for transfers between devices, body(): came = lax.ppermute(send, 'ci', flips[1])  3.73 us
    pallas_call x1, Pallas kernels, filter_terms(): pl.pallas_call(lambda *refs: filter_grad_kernel(*refs, scale=scale), out_...  2.65 us
    ppermute x1, starting transfers between devices, body(): bank_y = lax.ppermute(bank, 'co', other_y)  2.16 us
  transfers between devices with their start and end apart: 9, of which 6 were waited for; matrix products, arithmetic and copies ran while one was open for 0% of the time, Pallas kernels for 10%

profile of v3, /device:TPU:32, one launch (start us, length us, event | category | flops | bytes accessed | tf_op | source)
XLA Modules:
  0.0 55.1 jit_solution(12867523322204605359)
XLA Ops:
  0.6 0.0 copy-start.1
  0.6 0.7 %copy-done.1 = bf16[32,256]{1,0:T(8,128)(2,1)S(1)} copy-done((bf16[32,256]{1,0:T(8,128)(2,1)S(1)}, bf16[32,256]{1,0:T(8,128)(2,1)}, u32[]{:S(2)}) %copy-start.1) | copy-done | bytes 16408
  1.3 0.9 %pack.1 = bf16[16,64,128]{2,1,0:T(8,128)(2,1)} custom-call(bf16[32,256]{1,0:T(8,128)(2,1)S(1)} %copy-done.1), custom_call_target="tpu_custom_call" | custom-call | tf_op jit(solution)/shard_map/pack/pallas_call | solution.py:216
  2.2 0.0 copy-start
  2.2 8.3 %all-to-all-start = ((bf16[16,64,128]{2,1,0:T(8,128)(2,1)}), bf16[16,64,128]{2,1,0:T(8,128)(2,1)S(1)}, u32[]{:S(2)}, u32[]{:S(2)}) async-start(bf16[16,64,128]{2,1,0:T(8,128)(2,1)} %pack.1), calls=%async_computation | async-start | bytes 524288 | tf_op jit(solution)/shard_map/all_to_all | solution.py:308
  10.5 0.0 copy-done
  10.5 2.2 %collective-permute-start.5 = (bf16[27,32,128]{2,1,0:T(8,128)(2,1)S(1)}, bf16[27,32,128]{2,1,0:T(8,128)(2,1)S(1)}, u32[]{:S(2)}, u32[]{:S(2)}) collective-permute-start(bf16[27,32,128]{2,1,0:T(8,128)(2,1)S(1)} %copy-done), channel_id=1, source_target_pairs={{0,128},{8,136},{16,144},{24,152},{32,160},{40,168},{48,176},{56,1... | collective-permute-start | bytes 663560 | tf_op jit(solution)/shard_map/ppermute | solution.py:310
  12.7 8.5 %all-to-all-done = bf16[16,64,128]{2,1,0:T(8,128)(2,1)S(1)} async-done(((bf16[16,64,128]{2,1,0:T(8,128)(2,1)}), bf16[16,64,128]{2,1,0:T(8,128)(2,1)S(1)}, u32[]{:S(2)}, u32[]{:S(2)}) %all-to-all-start) | async-done | bytes 262176 | tf_op jit(solution)/shard_map/all_to_all | solution.py:308
  21.2 0.0 collective-permute-start.3
  21.2 0.5 collective-permute-start.4
  21.7 0.0 collective-permute-done.5.far_ref
  21.7 0.0 collective-permute-start.6
  21.7 0.7 %in_grad_terms.2.rest_0_ = f32[8,64,128]{2,1,0:T(8,128)S(1)} custom-call(bf16[2,8,64,128]{3,2,1,0:T(8,128)(2,1)S(1)} %bitcast.5, bf16[27,32,128]{2,1,0:T(8,128)(2,1)S(1)} %copy-done, bf16[27,32,128]{2,1,0:T(8,128)(2,1)S(1)} %collective-permute-done.5.far_ref), custom_call_target="tpu_custom_call" | custom-call | flops 226492416 | bytes 1000000 | tf_op jit(solution)/shard_map/in_grad_terms/pallas_call | solution.py:271
  22.4 0.6 %collective-permute-done.4.near_ref = bf16[27,32,128]{2,1,0:T(8,128)(2,1)S(1)} collective-permute-done((bf16[27,32,128]{2,1,0:T(8,128)(2,1)S(1)}, bf16[27,32,128]{2,1,0:T(8,128)(2,1)S(1)}, u32[]{:S(2)}, u32[]{:S(2)}) %collective-permute-start.4) | collective-permute-done | bytes 221216 | tf_op jit(solution)/shard_map/ppermute | solution.py:311
  23.0 0.3 collective-permute-done.6.far_ref
  23.3 0.0 collective-permute-done.3.grad_ref
  23.3 1.4 %in_grad_terms.3 = f32[8,64,128]{2,1,0:T(8,128)} custom-call(bf16[2,8,64,128]{3,2,1,0:T(8,128)(2,1)S(1)} %collective-permute-done.3.grad_ref, bf16[27,32,128]{2,1,0:T(8,128)(2,1)S(1)} %collective-permute-done.4.near_ref, bf16[27,32,128]{2,1,0:T(8,128)(2,1)S(1)} %collective-permute-done.6.far_ref, f32[8,64,128]{2,1,0:T(8,128)S(1)} %in_grad_terms.2.rest_0_), custom_call_target="tpu_custom_call" | custom-call | flops 226492416 | bytes 1000000 | tf_op jit(solution)/shard_map/in_grad_terms/pallas_call | solution.py:271
  24.8 0.0 copy-start.2
  24.8 9.3 %all-to-all-start.1 = ((f32[8,64,128]{2,1,0:T(8,128)}), f32[8,64,128]{2,1,0:T(8,128)S(1)}, u32[]{:S(2)}, u32[]{:S(2)}) async-start(f32[8,64,128]{2,1,0:T(8,128)} %in_grad_terms.3), calls=%async_computation.1 | async-start | bytes 524288 | tf_op jit(solution)/shard_map/all_to_all | solution.py:323
  34.1 0.0 copy-done.2
  34.1 1.6 %response_terms.1 = (f32[4,64,128]{2,1,0:T(8,128)S(1)}, f32[4,64,128]{2,1,0:T(8,128)S(1)}, bf16[1024,512]{1,0:T(8,128)(2,1)S(1)}) custom-call(bf16[128,2048]{1,0:T(8,128)(2,1)S(1)} %copy-done.2, bf16[27,32,128]{2,1,0:T(8,128)(2,1)S(1)} %copy-done), custom_call_target="tpu_custom_call" | custom-call | flops 452984832 | bytes 2000000 | tf_op jit(solution)/shard_map/response_terms/pallas_call | solution.py:229
  35.7 0.2 collective-permute-start
  35.9 5.2 %collective-permute-done.other_ref = f32[4,64,128]{2,1,0:T(8,128)S(1)} collective-permute-done((f32[4,64,128]{2,1,0:T(8,128)S(1)}, f32[4,64,128]{2,1,0:T(8,128)S(1)}, u32[]{:S(2)}, u32[]{:S(2)}) %collective-permute-start) | collective-permute-done | bytes 131104 | tf_op jit(solution)/shard_map/ppermute | solution.py:314
  41.1 0.8 %collective-permute-start.1 = (f32[2,64,128]{2,1,0:T(8,128)S(1)}, f32[2,64,128]{2,1,0:T(8,128)S(1)}, u32[]{:S(2)}, u32[]{:S(2)}) collective-permute-start(f32[2,64,128]{2,1,0:T(8,128)S(1)} %get-tuple-element.13), channel_id=1, source_target_pairs={{0,1},{1,0},{2,3},{3,2},{4,5},{5,4},{6,7},{7,6},{8,9},{9,8},{10,11... | collective-permute-start | bytes 196616 | tf_op jit(solution)/shard_map/ppermute | solution.py:316
  41.9 3.7 %collective-permute-done.1.other_ref = f32[2,64,128]{2,1,0:T(8,128)S(1)} collective-permute-done((f32[2,64,128]{2,1,0:T(8,128)S(1)}, f32[2,64,128]{2,1,0:T(8,128)S(1)}, u32[]{:S(2)}, u32[]{:S(2)}) %collective-permute-start.1) | collective-permute-done | bytes 65568 | tf_op jit(solution)/shard_map/ppermute | solution.py:316
  45.6 1.6 %collective-permute-start.2 = (f32[1,64,128]{2,1,0:T(8,128)S(1)}, f32[1,64,128]{2,1,0:T(8,128)S(1)}, u32[]{:S(2)}, u32[]{:S(2)}) collective-permute-start(f32[1,64,128]{2,1,0:T(8,128)S(1)} %get-tuple-element.15), channel_id=1, source_target_pairs={{0,2},{1,3},{2,0},{3,1},{4,6},{5,7},{6,4},{7,5},{8,10},{9,11},{10,... | collective-permute-start | bytes 98312 | tf_op jit(solution)/shard_map/ppermute | solution.py:318
  47.2 3.9 %collective-permute-done.2.other_ref = f32[1,64,128]{2,1,0:T(8,128)S(1)} collective-permute-done((f32[1,64,128]{2,1,0:T(8,128)S(1)}, f32[1,64,128]{2,1,0:T(8,128)S(1)}, u32[]{:S(2)}, u32[]{:S(2)}) %collective-permute-start.2) | collective-permute-done | bytes 32800 | tf_op jit(solution)/shard_map/ppermute | solution.py:318
  51.1 0.7 %response_out.1 = bf16[32,256]{1,0:T(8,128)(2,1)} custom-call(f32[1,64,128]{2,1,0:T(8,128)S(1)} %get-tuple-element.14.mine_ref, f32[1,64,128]{2,1,0:T(8,128)S(1)} %collective-permute-done.2.other_ref), custom_call_target="tpu_custom_call" | custom-call | tf_op jit(solution)/shard_map/response_out/pallas_call | solution.py:258
  51.8 2.7 %filter_terms.1 = f32[27,32,128]{2,1,0:T(8,128)} custom-call(bf16[2,8,64,128]{3,2,1,0:T(8,128)(2,1)S(1)} %bitcast.6, bf16[1024,512]{1,0:T(8,128)(2,1)S(1)} %get-tuple-element.16.refs_1_), custom_call_target="tpu_custom_call" | custom-call | flops 452984832 | bytes 2000000 | tf_op jit(solution)/shard_map/filter_terms/pallas_call | solution.py:284
  54.5 0.0 all-to-all-done.1
  54.5 0.6 %reduce_sum.9 = bf16[64,128]{1,0:T(8,128)(2,1)} reduce(f32[8,64,128]{2,1,0:T(8,128)S(1)} %all-to-all-done.1, f32[]{:T(128)} %constant.0.clone.1), dimensions={0}, to_apply=%region_0.0 | reduce | flops 57344 | bytes 278532 | tf_op jit(solution)/shard_map/reduce_sum | solution.py:324
  (2 shorter events, 0.0 us)
Async XLA Ops:
  0.6 0.7 %copy-start.1 = (bf16[32,256]{1,0:T(8,128)(2,1)S(1)}, bf16[32,256]{1,0:T(8,128)(2,1)}, u32[]{:S(2)}) copy-start(bf16[32,256]{1,0:T(8,128)(2,1)} %grad_ref.1) | copy-start | bytes 49156
  2.2 8.3 %copy-start = (bf16[27,32,128]{2,1,0:T(8,128)(2,1)S(1)}, bf16[27,32,128]{2,1,0:T(8,128)(2,1)}, u32[]{:S(2)}) copy-start(bf16[27,32,128]{2,1,0:T(8,128)(2,1)} %near_ref.1) | copy-start | bytes 663556
  2.2 19.0 %all-to-all-start = ((bf16[16,64,128]{2,1,0:T(8,128)(2,1)}), bf16[16,64,128]{2,1,0:T(8,128)(2,1)S(1)}, u32[]{:S(2)}, u32[]{:S(2)}) async-start(bf16[16,64,128]{2,1,0:T(8,128)(2,1)} %pack.1), calls=%async_computation | async-start | bytes 524288 | tf_op jit(solution)/shard_map/all_to_all | solution.py:308
  10.5 11.1 %collective-permute-start.5 = (bf16[27,32,128]{2,1,0:T(8,128)(2,1)S(1)}, bf16[27,32,128]{2,1,0:T(8,128)(2,1)S(1)}, u32[]{:S(2)}, u32[]{:S(2)}) collective-permute-start(bf16[27,32,128]{2,1,0:T(8,128)(2,1)S(1)} %copy-done), channel_id=1, source_target_pairs={{0,128},{8,136},{16,144},{24,152},{32,160},{40,168},{48,176},{56,1... | collective-permute-start | bytes 663560 | tf_op jit(solution)/shard_map/ppermute | solution.py:310
  21.2 2.2 %collective-permute-start.3 = (bf16[2,8,64,128]{3,2,1,0:T(8,128)(2,1)S(1)}, bf16[2,8,64,128]{3,2,1,0:T(8,128)(2,1)S(1)}, u32[]{:S(2)}, u32[]{:S(2)}) collective-permute-start(bf16[2,8,64,128]{3,2,1,0:T(8,128)(2,1)S(1)} %bitcast.4), channel_id=1, source_target_pairs={{0,8},{8,0},{16,24},{24,16},{32,40},{40,32},{48,56},{56,48},{64,72... | collective-permute-start | bytes 786440 | tf_op jit(solution)/shard_map/ppermute | solution.py:320
  21.2 1.8 %collective-permute-start.4 = (bf16[27,32,128]{2,1,0:T(8,128)(2,1)S(1)}, bf16[27,32,128]{2,1,0:T(8,128)(2,1)S(1)}, u32[]{:S(2)}, u32[]{:S(2)}) collective-permute-start(bf16[27,32,128]{2,1,0:T(8,128)(2,1)S(1)} %copy-done), channel_id=1, source_target_pairs={{0,8},{8,0},{16,24},{24,16},{32,40},{40,32},{48,56},{56,48},{64,72... | collective-permute-start | bytes 663560 | tf_op jit(solution)/shard_map/ppermute | solution.py:311
  21.7 1.7 %collective-permute-start.6 = (bf16[27,32,128]{2,1,0:T(8,128)(2,1)S(1)}, bf16[27,32,128]{2,1,0:T(8,128)(2,1)S(1)}, u32[]{:S(2)}, u32[]{:S(2)}) collective-permute-start(bf16[27,32,128]{2,1,0:T(8,128)(2,1)S(1)} %collective-permute-done.5.far_ref), channel_id=1, source_target_pairs={{0,8},{8,0},{16,24},{24,16},{32,40},{40,32},{48,56},{56,48},{64,72... | collective-permute-start | bytes 663560 | tf_op jit(solution)/shard_map/ppermute | solution.py:312
  24.8 9.3 %copy-start.2 = (bf16[128,2048]{1,0:T(8,128)(2,1)S(1)}, bf16[128,2048]{1,0:T(8,128)(2,1)}, u32[]{:S(2)}) copy-start(bf16[128,2048]{1,0:T(8,128)(2,1)} %x_ref.1) | copy-start | bytes 1572868
  24.8 29.7 %all-to-all-start.1 = ((f32[8,64,128]{2,1,0:T(8,128)}), f32[8,64,128]{2,1,0:T(8,128)S(1)}, u32[]{:S(2)}, u32[]{:S(2)}) async-start(f32[8,64,128]{2,1,0:T(8,128)} %in_grad_terms.3), calls=%async_computation.1 | async-start | bytes 524288 | tf_op jit(solution)/shard_map/all_to_all | solution.py:323
  35.7 5.3 %collective-permute-start = (f32[4,64,128]{2,1,0:T(8,128)S(1)}, f32[4,64,128]{2,1,0:T(8,128)S(1)}, u32[]{:S(2)}, u32[]{:S(2)}) collective-permute-start(f32[4,64,128]{2,1,0:T(8,128)S(1)} %get-tuple-element.11), channel_id=1, source_target_pairs={{0,4},{1,5},{2,6},{3,7},{4,0},{5,1},{6,2},{7,3},{8,12},{9,13},{10,... | collective-permute-start | bytes 393224 | tf_op jit(solution)/shard_map/ppermute | solution.py:314
  41.1 4.5 %collective-permute-start.1 = (f32[2,64,128]{2,1,0:T(8,128)S(1)}, f32[2,64,128]{2,1,0:T(8,128)S(1)}, u32[]{:S(2)}, u32[]{:S(2)}) collective-permute-start(f32[2,64,128]{2,1,0:T(8,128)S(1)} %get-tuple-element.13), channel_id=1, source_target_pairs={{0,1},{1,0},{2,3},{3,2},{4,5},{5,4},{6,7},{7,6},{8,9},{9,8},{10,11... | collective-permute-start | bytes 196616 | tf_op jit(solution)/shard_map/ppermute | solution.py:316
  45.6 5.5 %collective-permute-start.2 = (f32[1,64,128]{2,1,0:T(8,128)S(1)}, f32[1,64,128]{2,1,0:T(8,128)S(1)}, u32[]{:S(2)}, u32[]{:S(2)}) collective-permute-start(f32[1,64,128]{2,1,0:T(8,128)S(1)} %get-tuple-element.15), channel_id=1, source_target_pairs={{0,2},{1,3},{2,0},{3,1},{4,6},{5,7},{6,4},{7,5},{8,10},{9,11},{10,... | collective-permute-start | bytes 98312 | tf_op jit(solution)/shard_map/ppermute | solution.py:318
